TPU v7x, 256 devices: a whole 4x4x8 slice. The times are simulated.
256 devices in a mesh: dp: 8 (over x, y_lo), seq: 32 (over z, y_hi, core).
Axes of the slice: x: 4, y: 4 (y_hi: 2, y_lo: 2; y = y_hi * 2 + y_lo), z: 8, core: 2. Of those that a mesh axis runs over, the one named last changes fastest.
Arguments:
- video: bfloat16 [8, 32, 16, 160, 256], P('dp', 'seq'), may hold values from -6 to 6
- cotangent: bfloat16 [8, 32, 16, 160, 256], P('dp', 'seq'), may hold values from -6 to 6
- spatial_weight: bfloat16 [3, 3, 256, 256], replicated, may hold values from -0.125 to 0.125
- temporal_weight: bfloat16 [3, 256, 256], replicated, may hold values from -0.21875 to 0.21875
Outputs:
- video_grad: bfloat16 [8, 32, 16, 160, 256], P('dp', 'seq')
- spatial_grad: float32 [2304, 256], P('seq')
- temporal_grad: float32 [768, 256], P('seq')
All inputs are finite; a program needn't handle non-finite values.
Results may differ from a plain program's by a relative error of at most 0.0054.
Values may be sent and summed in bfloat16 or wider, within the bound.
A program may use at most 128 MiB of HBM per device.

v0:
```python
import jax
import jax.numpy as jnp
from jax import lax
from jax.sharding import PartitionSpec as P


def reduce_grads(partial_sum):
    whole = lax.psum(partial_sum, "dp")
    return lax.psum_scatter(whole, "seq", scatter_dimension=0, tiled=True)


def shards(video, cotangent, spatial_weight, temporal_weight):
    height, width, chans = (video.shape[2], video.shape[3], video.shape[4])
    positions = height * width
    frame = video[0, 0]
    padded = jnp.pad(frame, ((1, 1), (1, 1), (0, 0)))
    hidden = jnp.zeros((height, width, chans), jnp.float32)
    for a in range(3):
        for b in range(3):
            hidden = hidden + jnp.einsum(
                "hwc,cd->hwd",
                padded[a : a + height, b : b + width],
                spatial_weight[a, b],
                preferred_element_type=jnp.float32,
            )
    hidden_low = hidden.astype(jnp.bfloat16)
    grad_flat = cotangent[0, 0].reshape(1, positions, chans)
    hidden_flat = hidden_low.reshape(1, positions, chans)
    total_count = lax.axis_size("dp") * video.shape[0] * lax.axis_size("seq") * positions
    scale = 1.0 / jnp.sqrt(jnp.float32(total_count))
    grad_rows, hidden_rows = (
        lax.all_to_all(grad_flat, "seq", split_axis=1, concat_axis=0, tiled=True),
        lax.all_to_all(hidden_flat, "seq", split_axis=1, concat_axis=0, tiled=True),
    )
    frames = grad_rows.shape[0]
    hid32 = hidden_rows.astype(jnp.float32)
    sig = jax.nn.sigmoid(hid32)
    act = (hid32 * sig).astype(jnp.bfloat16)
    grad_pad = jnp.pad(grad_rows, ((0, 2), (0, 0), (0, 0)))
    act_grad = jnp.zeros(hid32.shape, jnp.float32)
    taps = []
    for k in range(3):
        act_grad = act_grad + jnp.einsum(
            "tqd,cd->tqc",
            grad_pad[k : k + frames],
            temporal_weight[k],
            preferred_element_type=jnp.float32,
        )
        taps.append(
            jnp.einsum(
                "tqc,tqd->cd", act[: frames - k], grad_rows[k:], preferred_element_type=jnp.float32
            )
        )
    temporal_part = jnp.concatenate(taps, axis=0)
    grad_rows_h = (act_grad * sig * (1.0 + hid32 * (1.0 - sig))).astype(jnp.bfloat16)
    back_flat = lax.all_to_all(grad_rows_h, "seq", split_axis=0, concat_axis=1, tiled=True)
    hidden_grad = back_flat.reshape(height, width, chans)
    temporal_grad = reduce_grads(temporal_part) * scale
    grad_pad2 = jnp.pad(hidden_grad, ((1, 1), (1, 1), (0, 0)))
    back = jnp.zeros((height, width, chans), jnp.float32)
    parts = []
    for a in range(3):
        for b in range(3):
            back = back + jnp.einsum(
                "hwd,cd->hwc",
                grad_pad2[2 - a : 2 - a + height, 2 - b : 2 - b + width],
                spatial_weight[a, b],
                preferred_element_type=jnp.float32,
            )
            parts.append(
                jnp.einsum(
                    "hwc,hwd->cd",
                    padded[a : a + height, b : b + width],
                    hidden_grad,
                    preferred_element_type=jnp.float32,
                )
            )
    spatial_grad = reduce_grads(jnp.concatenate(parts, axis=0)) * scale
    video_grad = back.astype(jnp.bfloat16).reshape(video.shape)
    return (video_grad, spatial_grad, temporal_grad)


def solution(mesh):
    placed = (P("dp", "seq", None, None, None), P("dp", "seq", None, None, None), P(), P())
    return jax.shard_map(
        shards,
        mesh=mesh,
        in_specs=placed,
        out_specs=(P("dp", "seq", None, None, None), P("seq", None), P("seq", None)),
        check_vma=False,
    )
```

profile of v0, /device:TPU:1, one launch (start us, length us, event | category | flops | bytes accessed | tf_op | source)
XLA Modules:
  0.0 474.9 jit_solution(2925747647652449)
XLA Ops:
  7.2 4.1 copy.19
  11.8 14.1 %reduce.1 = bf16[2560,256]{1,0:T(8,128)(2,1)} reduce(bf16[2560,1,256]{2,1,0:T(2,128)(2,1)S(1)} %bitcast.204, bf16[]{:T(256)} %broadcast.12), dimensions={1}, to_apply=%bitcast.159.reduce_sub_computation | reduce | bytes 2621442
  25.9 4.1 reshape.59
  30.0 12.9 %all-to-all-start = ((bf16[32,2,10240]{2,1,0:T(2,128)(2,1)}), bf16[32,2,10240]{2,1,0:T(2,128)(2,1)}, u32[]{:S(2)}, u32[]{:S(2)}) async-start(bf16[32,2,10240]{2,1,0:T(2,128)(2,1)} %reshape.59), calls=%async_computation | async-start | bytes 2621440 | tf_op jit(solution)/shard_map/all_to_all | solution.py:32
  47.1 2.2 add_convert_fusion.1
  49.3 16.0 %copy.18 = bf16[1,2560,256]{2,0,1:T(2,128)(2,1)} copy(bf16[1,2560,256]{2,1,0:T(8,128)(2,1)S(1)} %bitcast.206) | data formatting | bytes 2621440 | tf_op jit(solution)/shard_map/reshape | solution.py:28
  65.2 14.1 %reduce = bf16[2560,256]{1,0:T(8,128)(2,1)S(1)} reduce(bf16[2560,1,256]{2,1,0:T(2,128)(2,1)} %bitcast.205, bf16[]{:T(256)} %broadcast.12), dimensions={1}, to_apply=%bitcast.158.reduce_sub_computation | reduce | bytes 2621442
  80.6 9.9 %all-to-all-start.1 = ((bf16[32,2,10240]{2,1,0:T(2,128)(2,1)}), bf16[32,2,10240]{2,1,0:T(2,128)(2,1)}, u32[]{:S(2)}, u32[]{:S(2)}) async-start(bf16[32,2,10240]{2,1,0:T(2,128)(2,1)} %reshape.57), calls=%async_computation.1 | async-start | bytes 2621440 | tf_op jit(solution)/shard_map/all_to_all | solution.py:33
  90.4 8.9 %reshape.60 = bf16[2560,1,256]{2,1,0:T(2,128)(2,1)} reshape(bf16[32,2,10240]{2,1,0:T(2,128)(2,1)} %all-to-all-done) | data formatting | bytes 2621440
  105.4 18.5 %all-to-all-done.1 = bf16[32,2,10240]{2,1,0:T(2,128)(2,1)} async-done(((bf16[32,2,10240]{2,1,0:T(2,128)(2,1)}), bf16[32,2,10240]{2,1,0:T(2,128)(2,1)}, u32[]{:S(2)}, u32[]{:S(2)}) %all-to-all-start.1) | async-done | bytes 1310752 | tf_op jit(solution)/shard_map/all_to_all | solution.py:33
  123.9 8.9 %reshape.58 = bf16[2560,1,256]{2,1,0:T(2,128)(2,1)} reshape(bf16[32,2,10240]{2,1,0:T(2,128)(2,1)} %all-to-all-done.1) | data formatting | bytes 2621440
  132.8 2.1 copy.13
  136.8 2.4 multiply_convert_fusion.1
  139.2 6.1 %all-to-all-start.2 = ((bf16[32,80,256]{2,1,0:T(8,128)(2,1)}), bf16[32,80,256]{2,1,0:T(8,128)(2,1)S(1)}, u32[]{:S(2)}, u32[]{:S(2)}) async-start(bf16[32,80,256]{2,1,0:T(8,128)(2,1)} %multiply_convert_fusion.1), calls=%async_computation.2 | async-start | bytes 2621440 | tf_op jit(solution)/shard_map/all_to_all | solution.py:56
  145.3 4.9 %slice.165 = bf16[1,2480,256]{2,0,1:T(2,128)(2,1)S(1)} slice(bf16[1,2560,256]{2,0,1:T(2,128)(2,1)} %bitcast.195), slice={[0:1], [80:2560], [0:256]} | slice | bytes 2539520 | tf_op jit(solution)/shard_map/slice | solution.py:51
  150.2 2.6 slice.166
  159.2 19.7 %all-to-all-done.2 = bf16[32,80,256]{2,1,0:T(8,128)(2,1)S(1)} async-done(((bf16[32,80,256]{2,1,0:T(8,128)(2,1)}), bf16[32,80,256]{2,1,0:T(8,128)(2,1)S(1)}, u32[]{:S(2)}, u32[]{:S(2)}) %all-to-all-start.2) | async-done | bytes 1310752 | tf_op jit(solution)/shard_map/all_to_all | solution.py:56
  190.4 78.6 %reduce-scatter.5.cloned.1.call-done = f32[24,256]{1,0:T(8,128)} async-done(((f32[768,256]{1,0:T(8,128)}), f32[24,256]{1,0:T(8,128)}) %reduce-scatter.5.cloned.1.call-update) | async-done | bytes 24592 | tf_op jit(solution)/shard_map/reduce_scatter | solution.py:9
  269.0 26.7 %psum.17 = f32[24,256]{1,0:T(8,128)S(1)} all-reduce(f32[24,256]{1,0:T(8,128)} %reduce-scatter.5.cloned.1.call-done), channel_id=1, replica_groups=mesh['dp'=8,'seq'=32] {'dp'}, use_global_device_ids=true, to_apply=%region_2.3 | all-reduce | flops 6144 | bytes 49152 | tf_op jit(solution)/shard_map/psum | solution.py:8
  308.4 2.1 fusion.8
  310.5 2.1 fusion.82
  312.6 79.8 %reduce-scatter.3.cloned.1.call-done = f32[72,256]{1,0:T(8,128)} async-done(((f32[2304,256]{1,0:T(8,128)}), f32[72,256]{1,0:T(8,128)}) %reduce-scatter.3.cloned.1.call-update) | async-done | bytes 73744 | tf_op jit(solution)/shard_map/reduce_scatter | solution.py:9
  392.4 9.3 %fusion = bf16[1,1,16,160,256]{4,3,2,1,0:T(8,128)(2,1)} fusion(f32[16,160,256]{2,1,0:T(8,128)} %fusion.2, f32[16,160,256]{2,1,0:T(8,128)} %fusion.4, f32[16,160,256]{2,1,0:T(8,128)} %fusion.6, f32[16,160,256]{2,1,0:T(8,128)} %fusion.82, f32[16,160,256]{2,1,0:T(8,128)} %fusion.8, f32[16,160,256]{2,1,0:T(8,128)} %fusion.10, f32[16,160,256]{2,1,0:T(8,128)} %fusion.14, ...), kind=kOutput, calls=%fused_computation.5 | convolution fusion | flops 341442560 | bytes 23724032 | tf_op jit(solution)/shard_map/hwd,cd->hwc/dot_general | solution.py:64
  401.7 65.2 %all-reduce.5.cloned.1.call-done = f32[72,256]{1,0:T(8,128)} async-done(((f32[72,256]{1,0:T(8,128)}), f32[72,256]{1,0:T(8,128)}) %all-reduce.5.cloned.1.call-update) | async-done | bytes 73744 | tf_op jit(solution)/shard_map/psum | solution.py:8
  (66 shorter events, 45.9 us)
Async XLA Ops:
  30.0 13.0 %copy-start = (bf16[1,1,16,160,256]{4,3,2,1,0:T(8,128)(2,1)S(1)}, bf16[1,1,16,160,256]{4,3,2,1,0:T(8,128)(2,1)}, u32[]{:S(2)}) copy-start(bf16[1,1,16,160,256]{4,3,2,1,0:T(8,128)(2,1)} %param.4) | copy-start | bytes 3932164
  30.0 13.0 %copy-start.6 = (bf16[3,3,256,256]{3,2,1,0:T(8,128)(2,1)S(1)}, bf16[3,3,256,256]{3,2,1,0:T(8,128)(2,1)}, u32[]{:S(2)}) copy-start(bf16[3,3,256,256]{3,2,1,0:T(8,128)(2,1)} %param.6) | copy-start | bytes 3538948
  30.0 50.6 %all-to-all-start = ((bf16[32,2,10240]{2,1,0:T(2,128)(2,1)}), bf16[32,2,10240]{2,1,0:T(2,128)(2,1)}, u32[]{:S(2)}, u32[]{:S(2)}) async-start(bf16[32,2,10240]{2,1,0:T(2,128)(2,1)} %reshape.59), calls=%async_computation | async-start | bytes 2621440 | tf_op jit(solution)/shard_map/all_to_all | solution.py:32
  80.6 43.4 %all-to-all-start.1 = ((bf16[32,2,10240]{2,1,0:T(2,128)(2,1)}), bf16[32,2,10240]{2,1,0:T(2,128)(2,1)}, u32[]{:S(2)}, u32[]{:S(2)}) async-start(bf16[32,2,10240]{2,1,0:T(2,128)(2,1)} %reshape.57), calls=%async_computation.1 | async-start | bytes 2621440 | tf_op jit(solution)/shard_map/all_to_all | solution.py:33
  99.3 2.0 copy-start.10
  101.3 33.6 %copy-start.2 = (bf16[1,2560,256]{2,1,0:T(8,128)(2,1)}, bf16[1,2560,256]{2,1,0:T(8,128)(2,1)S(1)}, u32[]{:S(2)}) copy-start(bf16[1,2560,256]{2,1,0:T(8,128)(2,1)S(1)} %copy.12) | copy-start | bytes 3932164
  132.8 3.6 copy-start.8
  132.8 4.0 copy-start.9
  134.9 1.6 copy-start.4
  139.2 39.8 %all-to-all-start.2 = ((bf16[32,80,256]{2,1,0:T(8,128)(2,1)}), bf16[32,80,256]{2,1,0:T(8,128)(2,1)S(1)}, u32[]{:S(2)}, u32[]{:S(2)}) async-start(bf16[32,80,256]{2,1,0:T(8,128)(2,1)} %multiply_convert_fusion.1), calls=%async_computation.2 | async-start | bytes 2621440 | tf_op jit(solution)/shard_map/all_to_all | solution.py:56
  145.3 123.7 %reduce-scatter.5.cloned.1.call-start = ((), (), s32[]{:S(2)}) async-start(), calls=%async_computation.7 | async-start | bytes 811008 | tf_op jit(solution)/shard_map/reduce_scatter | solution.py:9
  145.3 4.9 %copy-start.1 = (bf16[2560,1,256]{2,1,0:T(2,128)(2,1)S(1)}, bf16[2560,1,256]{2,1,0:T(2,128)(2,1)}, u32[]{:S(2)}) copy-start(bf16[2560,1,256]{2,1,0:T(2,128)(2,1)} %reshape.60) | copy-start | bytes 3932164
  153.1 1.7 copy-start.5
  156.1 1.3 copy-start.3
  158.9 233.4 %reduce-scatter.3.cloned.1.call-start = ((), (), s32[]{:S(2)}) async-start(), calls=%async_computation.5 | async-start | bytes 2433024 | tf_op jit(solution)/shard_map/reduce_scatter | solution.py:9
  190.3 105.9 %copy-start.7 = (bf16[3,3,256,256]{3,2,1,0:T(8,128)(2,1)S(1)}, bf16[3,3,256,256]{3,2,1,0:T(8,128)(2,1)}, u32[]{:S(2)}) copy-start(bf16[3,3,256,256]{3,2,1,0:T(8,128)(2,1)} %param.6) | copy-start | bytes 3538948
  190.4 276.5 %all-reduce.5.cloned.1.call-start = ((), (), s32[]{:S(2)}) async-start(), calls=%async_computation.6 | async-start | bytes 147456 | tf_op jit(solution)/shard_map/psum | solution.py:8
Sparse Core Ops, SparseCore 0:
  159.1 109.8 reduce-scatter.4
  273.7 118.6 reduce-scatter.2
  395.0 71.8 all-reduce.4
where the time goes:
time: 480 us; the launch traced here: 475 us
  waiting for transfers between devices  262 us (55%)
  local copies, waits for them, and re-layouts  59.8 us (12%)
  matrix products  51.3 us (11%)
  other arithmetic  32.1 us (7%)
  starting transfers between devices  29.3 us (6%)
  blocking collectives  26.7 us (6%)
  between operations  14 us (3%)
    reduce_scatter x2, waiting for transfers between devices, reduce_grads(): return lax.psum_scatter(whole, 'seq', scatter_dimension=0, tiled=True)  158 us
    psum x1, waiting for transfers between devices, reduce_grads(): whole = lax.psum(partial_sum, 'dp')  65.2 us
    unnamed x31, local copies, waits for them, and re-layouts  32.3 us
    unnamed x2, other arithmetic  28.3 us
    psum x1, blocking collectives, reduce_grads(): whole = lax.psum(partial_sum, 'dp')  26.7 us
    dot_general x9, matrix products, shards(): jnp.einsum('hwd,cd->hwc', grad_pad2[2 - a:2 - a + height, 2 - b:2 - b + w...  25.6 us
    all_to_all x1, waiting for transfers between devices, shards(): lax.all_to_all(grad_rows_h, 'seq', split_axis=0, concat_axis=1, tiled=True)  19.7 us
    all_to_all x1, waiting for transfers between devices, shards(): lax.all_to_all(hidden_flat, 'seq', split_axis=1, concat_axis=0, tiled=True)  18.5 us
  transfers between devices with their start and end apart: 6, of which 5 were waited for; matrix products, arithmetic and copies ran while one was open for 21% of the time, Pallas kernels for 0%

commit v1 on v0

v1 whole, which is shorter than its diff:
```python
import functools
import jax
import jax.numpy as jnp
from jax import lax
from jax.sharding import PartitionSpec as P
from jax.experimental import pallas as pl
from jax.experimental.pallas import tpu as pltpu

MESH = pl.DeviceIdType.MESH
H, W, C = 16, 160, 256
POS = H * W
NQ = 8
RQ = POS // NQ
F32, BF16 = jnp.float32, jnp.bfloat16


def dot(a, b):
    return lax.dot_general(a, b, (((1,), (0,)), ((), ())), preferred_element_type=F32)


def shifted(x):
    n = x.shape[0]
    col = lax.broadcasted_iota(jnp.int32, x.shape, 0) % W
    before = jnp.where(col == 0, 0.0, pltpu.roll(x, 1, 0))
    after = jnp.where(col == W - 1, 0.0, pltpu.roll(x, n - 1, 0))
    return before, after


def body(v_ref, c_ref, sw_ref, tw_ref, vg_ref, g_ref, vcat, hgcat, cots, v_t, a_t, dsil, sw_t, tw_t,
         far_send, far_recv, near_send, near_recv):
    seq = lax.axis_index("seq")
    n_seq = lax.axis_size("seq")
    core = lax.rem(seq, 2)
    sibling = seq + 1 - 2 * core
    prev = lax.rem(seq + n_seq - 2, n_seq)
    following = lax.rem(seq + 2, n_seq)

    def rows(q):
        return pl.ds(pl.multiple_of(q * RQ, RQ), RQ)

    def far(q):
        return pltpu.make_async_remote_copy(
            src_ref=c_ref.at[rows(q)], dst_ref=cots.at[rows(q), pl.ds(2 * C, C)],
            send_sem=far_send.at[q], recv_sem=far_recv.at[q],
            device_id={"seq": prev}, device_id_type=MESH)

    def near_own(q):
        return pltpu.make_async_remote_copy(
            src_ref=c_ref.at[rows(q)], dst_ref=cots.at[rows(q), pl.ds(C, C)],
            send_sem=near_send.at[q], recv_sem=near_recv.at[q],
            device_id={"seq": sibling}, device_id_type=MESH)

    def near_pass(q):
        return pltpu.make_async_remote_copy(
            src_ref=cots.at[rows(q), pl.ds(2 * C, C)], dst_ref=cots.at[rows(q), pl.ds(C, C)],
            send_sem=near_send.at[q], recv_sem=near_recv.at[q],
            device_id={"seq": sibling}, device_id_type=MESH)

    barrier = pltpu.get_barrier_semaphore()
    for other in (following, sibling):
        pl.semaphore_signal(barrier, inc=1, device_id={"seq": other}, device_id_type=MESH)
    pl.semaphore_wait(barrier, 2)
    for q in range(NQ):
        far(q).start()

    @pl.when(core == 1)
    def _():
        for q in range(NQ):
            near_own(q).start()

    for a in range(3):
        for b in range(3):
            sw_t[a, b * C:(b + 1) * C, :] = sw_ref[a, b * C:(b + 1) * C, :].T
        live = (seq + a < n_seq).astype(F32)
        tw_t[a * C:(a + 1) * C, :] = (tw_ref[a].astype(F32) * live).astype(BF16).T

    zero = jnp.zeros((W, 3 * C), BF16)
    for ref in (vcat, hgcat):
        ref[0:W, :] = zero
        ref[W + POS:2 * W + POS, :] = zero

    def load(q, _):
        x = v_ref[rows(q), :]
        before, after = shifted(x.astype(F32))
        out = pl.ds(pl.multiple_of(W + q * RQ, W), RQ)
        vcat[out, 0:C] = before.astype(BF16)
        vcat[out, C:2 * C] = x
        vcat[out, 2 * C:] = after.astype(BF16)
        cots[rows(q), 0:C] = c_ref[rows(q), :]
        return 0
    lax.fori_loop(0, NQ, load, 0)
    for m in range(POS // C):
        v_t[:, m * C:(m + 1) * C] = v_ref[m * C:(m + 1) * C, :].T

    def forward(q, _):
        acc = jnp.zeros((RQ, C), F32)
        for a in range(3):
            acc = acc + dot(vcat[pl.ds(pl.multiple_of(q * RQ + a * W, W), RQ), :], sw_ref[a])
        v = acc.astype(BF16).astype(F32)
        s = 1.0 / (1.0 + jnp.exp(-v))
        dsil[rows(q), :] = s * (1.0 + v * (1.0 - s))
        hgcat[pl.ds(pl.multiple_of(W + q * RQ, W), RQ), 0:C] = (v * s).astype(BF16)
        return 0
    lax.fori_loop(0, NQ, forward, 0)
    for m in range(POS // C):
        a_t[:, m * C:(m + 1) * C] = hgcat[W + m * C:W + (m + 1) * C, 0:C].T

    def chunk(q, _):
        far(q).wait_recv()

        @pl.when(core == 0)
        def _():
            near_pass(q).start()
        near_own(q).wait_recv()
        grad = dot(cots[rows(q), :], tw_t[...])
        hg = (grad * dsil[rows(q), :]).astype(BF16)
        before, after = shifted(hg.astype(F32))
        out = pl.ds(pl.multiple_of(W + q * RQ, W), RQ)
        hgcat[out, 0:C] = after.astype(BF16)
        hgcat[out, C:2 * C] = hg
        hgcat[out, 2 * C:] = before.astype(BF16)
        return 0

    def put(first, index, part):
        for b in range(3):
            where = pl.ds(pl.multiple_of((index * 3 + b) * C, C), C)
            value = part[:, b * C:(b + 1) * C]
            g_ref[where, :] = value if first else g_ref[where, :] + value

    def grads(start, size, first):
        def tap(a, _):
            from_row = pl.multiple_of(start + (2 - a) * W, 32)
            put(first, a, dot(v_t[:, start:start + size], hgcat[pl.ds(from_row, size), :]))
            return 0
        lax.fori_loop(0, 3, tap, 0)
        put(first, 3, dot(a_t[:, start:start + size], cots[start:start + size, :]))

    lax.fori_loop(0, 4, chunk, 0)
    grads(0, 1024, True)
    lax.fori_loop(4, 6, chunk, 0)
    grads(1024, 512, False)
    lax.fori_loop(6, 7, chunk, 0)
    grads(1536, 512, False)
    lax.fori_loop(7, 8, chunk, 0)
    grads(2048, 512, False)
    for k in (1, 2):
        live = (seq + k < n_seq).astype(F32)
        where = slice((9 + k) * C, (10 + k) * C)
        g_ref[where, :] = g_ref[where, :] * live

    def back(q, _):
        acc = jnp.zeros((RQ, C), F32)
        for a in range(3):
            acc = acc + dot(hgcat[pl.ds(pl.multiple_of(q * RQ + (2 - a) * W, W), RQ), :], sw_t[a])
        vg_ref[rows(q), :] = acc.astype(BF16)
        return 0
    lax.fori_loop(0, NQ, back, 0)

    def drain(q, _):
        far(q).wait_send()
        near_own(q).wait_send()
        return 0
    lax.fori_loop(0, NQ, drain, 0)


def compute(v, c, sw, tw):
    vm = pl.BlockSpec(memory_space=pltpu.VMEM)
    return pl.pallas_call(
        body, name="halo_conv",
        out_shape=(jax.ShapeDtypeStruct((POS, C), BF16), jax.ShapeDtypeStruct((12 * C, C), F32)),
        in_specs=[vm] * 4, out_specs=(vm, vm),
        scratch_shapes=[
            pltpu.VMEM((POS + 2 * W, 3 * C), BF16),
            pltpu.VMEM((POS + 2 * W, 3 * C), BF16),
            pltpu.VMEM((POS, 3 * C), BF16),
            pltpu.VMEM((C, POS), BF16),
            pltpu.VMEM((C, POS), BF16),
            pltpu.VMEM((POS, C), F32),
            pltpu.VMEM((3, 3 * C, C), BF16),
            pltpu.VMEM((3 * C, C), BF16),
        ] + [pltpu.SemaphoreType.DMA((NQ,))] * 4,
        compiler_params=pltpu.CompilerParams(
            collective_id=0, has_side_effects=True, vmem_limit_bytes=56 * 2**20),
    )(v, c, sw, tw)


def shards(video, cotangent, spatial_weight, temporal_weight):
    vg, g = compute(video.reshape(POS, C), cotangent.reshape(POS, C),
                    spatial_weight.reshape(3, 3 * C, C), temporal_weight)
    scale = 1.0 / jnp.sqrt(jnp.float32(8 * 32 * POS))
    g = lax.psum_scatter(jnp.concatenate([g[:9 * C].reshape(32, 72, C), g[9 * C:].reshape(32, 24, C)], axis=1).reshape(12 * C, C),
                         "seq", scatter_dimension=0, tiled=True)
    g = lax.psum(g, "dp") * scale
    return vg.reshape(video.shape), g[:72], g[72:]


def solution(mesh):
    placed = (P("dp", "seq", None, None, None), P("dp", "seq", None, None, None), P(), P())
    return jax.shard_map(
        shards, mesh=mesh, in_specs=placed,
        out_specs=(P("dp", "seq", None, None, None), P("seq", None), P("seq", None)),
        check_vma=False)
```

time: 480 us -> 271 us (0.56)
  waiting for transfers between devices: 262 us -> 198 us
  local copies, waits for them, and re-layouts: 59.8 us -> 5.31 us
  matrix products: 51.3 us -> 0 us
  Pallas kernels: 0 us -> 46.3 us
  starting transfers between devices: 29.3 us -> 0.08 us
  other arithmetic: 32.1 us -> 2.98 us
  blocking collectives: 26.7 us -> 0 us
    dot_general x33 -> x0, matrix products: 51.3 us -> none  [the longest x9 25.6 us: shards(): jnp.einsum('hwd,cd->hwc', grad_pad2[2 - a:2 - a + height, 2 - b:2 - b + w...]
    pallas_call x0 -> x1, Pallas kernels: none -> 46.3 us  [compute(): pl.pallas_call(body, name='halo_conv', out_shape=(jax.ShapeDtypeStruct((P...]
    all_to_all x3 -> x0, waiting for transfers between devices: 38.3 us -> none  [the longest x1 19.7 us: shards(): lax.all_to_all(grad_rows_h, 'seq', split_axis=0, concat_axis=1, tiled=True)]
    reduce_scatter x2 -> x1, waiting for transfers between devices: 158 us -> 120 us  [shards(): lax.psum_scatter(jnp.concatenate([g[:9 * C].reshape(32, 72, C), g[9 * C:]...]
    unnamed x31 -> x3, local copies, waits for them, and re-layouts: 32.3 us -> 1.06 us
    all_to_all x3 -> x0, starting transfers between devices: 28.9 us -> none  [the longest x1 12.9 us: shards(): lax.all_to_all(grad_flat, 'seq', split_axis=1, concat_axis=0, tiled=True)]
    unnamed x2 -> x0, other arithmetic: 28.3 us -> none
    psum x1 -> x0, blocking collectives: 26.7 us -> none  [reduce_grads(): whole = lax.psum(partial_sum, 'dp')]
  transfers between devices with their start and end apart: 6 -> 2, of which waited for: 5 -> 2; matrix products, arithmetic and copies ran while one was open for 21% -> 0% of each run, Pallas kernels for 0% -> 0%
where the time goes in v1:
time: 271 us; the launch traced here: 267 us
  waiting for transfers between devices  198 us (73%)
  Pallas kernels  46.3 us (17%)
  between operations  14.1 us (5%)
  local copies, waits for them, and re-layouts  5.31 us (2%)
  other arithmetic  2.98 us (1%)
    reduce_scatter x1, waiting for transfers between devices, shards(): lax.psum_scatter(jnp.concatenate([g[:9 * C].reshape(32, 72, C), g[9 * C:]...  120 us
    psum x1, waiting for transfers between devices, shards(): g = lax.psum(g, 'dp') * scale  77.6 us
    pallas_call x1, Pallas kernels, compute(): pl.pallas_call(body, name='halo_conv', out_shape=(jax.ShapeDtypeStruct((P...  46.3 us
  transfers between devices with their start and end apart: 2, of which 2 were waited for; matrix products, arithmetic and copies ran while one was open for 0% of the time, Pallas kernels for 0%

profile of v1, /device:TPU:1, one launch (start us, length us, event | category | flops | bytes accessed | tf_op | source)
XLA Modules:
  0.0 266.8 jit_solution(10738954800149262400)
XLA Ops:
  7.2 0.0 reduce-scatter.2.cloned.1.call-start
  7.2 46.3 %halo_conv.1 = (bf16[2560,256]{1,0:T(8,128)(2,1)}, f32[3072,256]{1,0:T(8,128)}) custom-call(bf16[2560,256]{1,0:T(8,128)(2,1)} %bitcast.10, bf16[2560,256]{1,0:T(8,128)(2,1)} %bitcast.11, bf16[3,768,256]{2,1,0:T(8,128)(2,1)} %bitcast.13, bf16[3,256,256]{2,1,0:T(8,128)(2,1)} %tw_ref.1), custom_call_target="tpu_custom_call" | custom-call | tf_op jit(solution)/shard_map/halo_conv/pallas_call | solution.py:168
  53.5 1.2 slice.13
  54.7 1.8 slice.12
  56.5 2.1 pad_maximum_fusion
  58.6 0.0 copy-start
  58.6 0.0 reduce-scatter.2.cloned.1.call-update
  58.6 0.0 all-reduce.2.cloned.1.call-start
  58.7 120.5 %reduce-scatter.2.cloned.1.call-done = f32[96,256]{1,0:T(8,128)} async-done(((f32[3072,256]{1,0:T(8,128)}), f32[96,256]{1,0:T(8,128)}) %reduce-scatter.2.cloned.1.call-update) | async-done | bytes 98320 | tf_op jit(solution)/shard_map/reduce_scatter | solution.py:191
  179.1 0.0 all-reduce.2.cloned.1.call-update
  179.2 77.6 %all-reduce.2.cloned.1.call-done = f32[96,256]{1,0:T(8,128)} async-done(((f32[96,256]{1,0:T(8,128)}), f32[96,256]{1,0:T(8,128)}) %all-reduce.2.cloned.1.call-update) | async-done | bytes 98320 | tf_op jit(solution)/shard_map/psum | solution.py:193
  256.8 0.9 broadcast_multiply_fusion
  257.7 0.6 slice.17
  258.3 0.6 slice.16
  258.9 0.0 copy-done
  258.9 1.1 copy.9
Async XLA Ops:
  7.2 172.0 %reduce-scatter.2.cloned.1.call-start = ((), (), s32[]{:S(2)}) async-start(), calls=%async_computation.1 | async-start | bytes 3244032 | tf_op jit(solution)/shard_map/reduce_scatter | solution.py:191
  58.6 200.3 %copy-start = (bf16[2560,256]{1,0:T(8,128)(2,1)S(1)}, bf16[2560,256]{1,0:T(8,128)(2,1)}, u32[]{:S(2)}) copy-start(bf16[2560,256]{1,0:T(8,128)(2,1)} %get-tuple-element.5) | copy-start | bytes 3932164
  58.6 198.2 %all-reduce.2.cloned.1.call-start = ((), (), s32[]{:S(2)}) async-start(), calls=%async_computation.2 | async-start | bytes 196608 | tf_op jit(solution)/shard_map/psum | solution.py:193
Sparse Core Ops, SparseCore 0:
  58.7 120.3 reduce-scatter.1
  182.0 74.7 all-reduce.1

commit v2 on v1

--- a/solution.py
+++ b/solution.py
@@ -26,8 +26,10 @@
     return before, after
 
 
-def body(v_ref, c_ref, sw_ref, tw_ref, vg_ref, g_ref, vcat, hgcat, cots, v_t, a_t, dsil, sw_t, tw_t,
-         far_send, far_recv, near_send, near_recv):
+def body(scale, v_ref, c_ref, sw_ref, tw_ref, vg_ref, sg_ref, tg_ref,
+         vcat, hgcat, cots, v_t, a_t, dsil, sw_t, tw_t, g_ref,
+         pair_out, pair_in, a1_out, a1_in, a2_out, a2_in, b1_out, b1_in, b2_out, b2_in, last_out, last_in,
+         far_send, far_recv, near_send, near_recv, pair_sems, a1_sems, a2_sems, b1_sems, b2_sems, last_send, last_recv):
     seq = lax.axis_index("seq")
     n_seq = lax.axis_size("seq")
     core = lax.rem(seq, 2)
@@ -56,10 +58,24 @@
             send_sem=near_send.at[q], recv_sem=near_recv.at[q],
             device_id={"seq": sibling}, device_id_type=MESH)
 
+    dp = lax.axis_index("dp")
+    x, y_lo = dp // 2, lax.rem(dp, 2)
+    z, y_hi = seq // 4, lax.rem(seq // 2, 2)
+    y = 2 * y_hi + y_lo
+
+    def place(dx, dy, dz):
+        to_x, to_y, to_z = lax.rem(x + dx, 4), lax.rem(y + dy, 4), lax.rem(z + dz, 8)
+        return (2 * to_x + lax.rem(to_y, 2), 4 * to_z + 2 * (to_y // 2) + core)
+
+    plane = [(dx, dy) for dx in range(4) for dy in range(4) if dx or dy]
     barrier = pltpu.get_barrier_semaphore()
     for other in (following, sibling):
         pl.semaphore_signal(barrier, inc=1, device_id={"seq": other}, device_id_type=MESH)
-    pl.semaphore_wait(barrier, 2)
+    for dx, dy in plane:
+        pl.semaphore_signal(barrier, inc=1, device_id=place(dx, dy, 0), device_id_type=MESH)
+    for dz in range(1, 8):
+        pl.semaphore_signal(barrier, inc=1, device_id=place(0, 0, dz), device_id_type=MESH)
+    pl.semaphore_wait(barrier, 24)
     for q in range(NQ):
         far(q).start()
 
@@ -143,18 +159,152 @@
     grads(1536, 512, False)
     lax.fori_loop(7, 8, chunk, 0)
     grads(2048, 512, False)
-    for k in (1, 2):
-        live = (seq + k < n_seq).astype(F32)
-        where = slice((9 + k) * C, (10 + k) * C)
-        g_ref[where, :] = g_ref[where, :] * live
-
     def back(q, _):
         acc = jnp.zeros((RQ, C), F32)
         for a in range(3):
             acc = acc + dot(hgcat[pl.ds(pl.multiple_of(q * RQ + (2 - a) * W, W), RQ), :], sw_t[a])
         vg_ref[rows(q), :] = acc.astype(BF16)
         return 0
-    lax.fori_loop(0, NQ, back, 0)
+    def own(g, parity):
+        return (pl.ds(pl.multiple_of(144 * g + 72 * parity, 8), 72),
+                pl.ds(pl.multiple_of(9 * C + 48 * g + 24 * parity, 8), 24))
+
+    def masked(g, parity):
+        row = 48 * g + 24 * parity + lax.broadcasted_iota(jnp.int32, (24, C), 0)
+        tap = row // C
+        return jnp.where(seq + tap < n_seq, 1.0, 0.0)
+
+    def give(g, _):
+        s_rows, t_rows = own(g, 1 - core)
+        pair_out[g, 0:72, :] = g_ref[s_rows, :].astype(BF16)
+        pair_out[g, 72:96, :] = (g_ref[t_rows, :] * masked(g, 1 - core)).astype(BF16)
+        return 0
+    lax.fori_loop(0, 16, give, 0)
+    pair = pltpu.make_async_remote_copy(
+        src_ref=pair_out, dst_ref=pair_in, send_sem=pair_sems.at[0], recv_sem=pair_sems.at[1],
+        device_id={"seq": sibling}, device_id_type=MESH)
+    pair.start()
+    lax.fori_loop(0, 1, back, 0)
+    pair.wait_recv()
+
+    def take(g, _):
+        s_rows, t_rows = own(g, core)
+        s_sum = g_ref[s_rows, :] + pair_in[g, 0:72, :].astype(F32)
+        t_sum = g_ref[t_rows, :] * masked(g, core) + pair_in[g, 72:96, :].astype(F32)
+        a1_out[g, :, :] = s_sum[0:64].astype(BF16)
+        b1_out[g, 0:8, :] = s_sum[64:72].astype(BF16)
+        b1_out[g, 8:32, :] = t_sum.astype(BF16)
+        return 0
+    lax.fori_loop(0, 16, take, 0)
+
+    def quarter(at):
+        return pl.ds(pl.multiple_of(16 * at, 16), 16)
+
+    def a1(d):
+        return pltpu.make_async_remote_copy(
+            src_ref=a1_out.at[:, quarter(lax.rem(x + d, 4)), :], dst_ref=a1_in.at[d - 1],
+            send_sem=a1_sems.at[0, d - 1], recv_sem=a1_sems.at[1, d - 1],
+            device_id=place(d, 0, 0), device_id_type=MESH)
+
+    def b1(d):
+        return pltpu.make_async_remote_copy(
+            src_ref=b1_out.at[pl.ds(2 * lax.rem(z + d, 8), 2)], dst_ref=b1_in.at[d - 1],
+            send_sem=b1_sems.at[0, d - 1], recv_sem=b1_sems.at[1, d - 1],
+            device_id=place(0, 0, d), device_id_type=MESH)
+
+    def a2(d):
+        return pltpu.make_async_remote_copy(
+            src_ref=a2_out.at[pl.ds(2 * lax.rem(z + d, 8), 2)], dst_ref=a2_in.at[d - 1],
+            send_sem=a2_sems.at[0, d - 1], recv_sem=a2_sems.at[1, d - 1],
+            device_id=place(0, 0, d), device_id_type=MESH)
+
+    def b2(d):
+        return pltpu.make_async_remote_copy(
+            src_ref=b2_out.at[lax.rem(x + d, 4)], dst_ref=b2_in.at[d - 1],
+            send_sem=b2_sems.at[0, d - 1], recv_sem=b2_sems.at[1, d - 1],
+            device_id=place(d, 0, 0), device_id_type=MESH)
+
+    for d in range(1, 4):
+        a1(d).start()
+    for d in range(1, 8):
+        b1(d).start()
+    lax.fori_loop(1, 5, back, 0)
+    for d in range(1, 8):
+        b1(d).wait_recv()
+    b_sum = b1_out[pl.ds(2 * z, 2), :, :].astype(F32)
+    for d in range(1, 8):
+        b_sum = b_sum + b1_in[d - 1].astype(F32)
+    for q in range(4):
+        b2_out[q, :, :, :] = b_sum[:, 8 * q:8 * q + 8, :]
+    for d in range(1, 4):
+        b2(d).start()
+    for d in range(1, 4):
+        a1(d).wait_recv()
+
+    def a_add(g, _):
+        total = a1_out[g, quarter(x), :].astype(F32)
+        for d in range(3):
+            total = total + a1_in[d, g, :, :].astype(F32)
+        a2_out[g, :, :] = total.astype(BF16)
+        return 0
+    lax.fori_loop(0, 16, a_add, 0)
+    for d in range(1, 8):
+        a2(d).start()
+    lax.fori_loop(5, 7, back, 0)
+    for d in range(1, 4):
+        b2(d).wait_recv()
+    b_sum = b2_out[x, :, :, :]
+    for d in range(3):
+        b_sum = b_sum + b2_in[d]
+    for d in range(1, 8):
+        a2(d).wait_recv()
+    a_sum = a2_out[pl.ds(2 * z, 2), :, :].astype(F32)
+    for d in range(7):
+        a_sum = a_sum + a2_in[d].astype(F32)
+    last_out[:, 0:16, :] = a_sum.astype(BF16)
+    last_out[:, 16:24, :] = b_sum.astype(BF16)
+    me = 4 * x + y
+
+    def last(n):
+        dx, dy = plane[n]
+        return pltpu.make_async_remote_copy(
+            src_ref=last_out.at[lax.rem(y + dy, 4) // 2], dst_ref=last_in.at[me],
+            send_sem=last_send.at[n], recv_sem=last_recv.at[me],
+            device_id=place(dx, dy, 0), device_id_type=MESH)
+
+    def last_from(n):
+        dx, dy = plane[n]
+        other = 4 * lax.rem(x + dx, 4) + lax.rem(y + dy, 4)
+        return pltpu.make_async_remote_copy(
+            src_ref=last_out.at[0], dst_ref=last_in.at[other],
+            send_sem=last_send.at[n], recv_sem=last_recv.at[other],
+            device_id=place(dx, dy, 0), device_id_type=MESH)
+
+    for n in range(15):
+        last(n).start()
+    last_in[me, :, :] = last_out[y_hi, :, :]
+    lax.fori_loop(7, NQ, back, 0)
+    for n in range(15):
+        last_from(n).wait_recv()
+    for q in range(4):
+        total = last_in[4 * q].astype(F32)
+        for k in range(1, 4):
+            total = total + last_in[4 * q + k].astype(F32)
+        total = total * scale
+        sg_ref[16 * q:16 * q + 16, :] = total[0:16]
+        if q == 0:
+            sg_ref[64:72, :] = total[16:24]
+        else:
+            tg_ref[8 * q - 8:8 * q, :] = total[16:24]
+    pair.wait_send()
+    for d in range(1, 4):
+        a1(d).wait_send()
+        b2(d).wait_send()
+    for d in range(1, 8):
+        b1(d).wait_send()
+        a2(d).wait_send()
+    for n in range(15):
+        last(n).wait_send()
 
     def drain(q, _):
         far(q).wait_send()
@@ -163,12 +313,14 @@
     lax.fori_loop(0, NQ, drain, 0)
 
 
-def compute(v, c, sw, tw):
+def compute(v, c, sw, tw, scale):
     vm = pl.BlockSpec(memory_space=pltpu.VMEM)
+    dma = pltpu.SemaphoreType.DMA
     return pl.pallas_call(
-        body, name="halo_conv",
-        out_shape=(jax.ShapeDtypeStruct((POS, C), BF16), jax.ShapeDtypeStruct((12 * C, C), F32)),
-        in_specs=[vm] * 4, out_specs=(vm, vm),
+        functools.partial(body, scale), name="halo_conv",
+        out_shape=(jax.ShapeDtypeStruct((POS, C), BF16), jax.ShapeDtypeStruct((72, C), F32),
+                   jax.ShapeDtypeStruct((24, C), F32)),
+        in_specs=[vm] * 4, out_specs=(vm, vm, vm),
         scratch_shapes=[
             pltpu.VMEM((POS + 2 * W, 3 * C), BF16),
             pltpu.VMEM((POS + 2 * W, 3 * C), BF16),
@@ -178,20 +330,24 @@
             pltpu.VMEM((POS, C), F32),
             pltpu.VMEM((3, 3 * C, C), BF16),
             pltpu.VMEM((3 * C, C), BF16),
-        ] + [pltpu.SemaphoreType.DMA((NQ,))] * 4,
+            pltpu.VMEM((12 * C, C), F32),
+            pltpu.VMEM((16, 96, C), BF16), pltpu.VMEM((16, 96, C), BF16),
+            pltpu.VMEM((16, 64, C), BF16), pltpu.VMEM((3, 16, 16, C), BF16),
+            pltpu.VMEM((16, 16, C), BF16), pltpu.VMEM((7, 2, 16, C), BF16),
+            pltpu.VMEM((16, 32, C), BF16), pltpu.VMEM((7, 2, 32, C), BF16),
+            pltpu.VMEM((4, 2, 8, C), F32), pltpu.VMEM((3, 2, 8, C), F32),
+            pltpu.VMEM((2, 24, C), BF16), pltpu.VMEM((16, 24, C), BF16),
+        ] + [dma((NQ,))] * 4 + [dma((2,)), dma((2, 3)), dma((2, 7)), dma((2, 7)), dma((2, 3)), dma((15,)), dma((16,))],
         compiler_params=pltpu.CompilerParams(
             collective_id=0, has_side_effects=True, vmem_limit_bytes=56 * 2**20),
     )(v, c, sw, tw)
 
 
 def shards(video, cotangent, spatial_weight, temporal_weight):
-    vg, g = compute(video.reshape(POS, C), cotangent.reshape(POS, C),
-                    spatial_weight.reshape(3, 3 * C, C), temporal_weight)
-    scale = 1.0 / jnp.sqrt(jnp.float32(8 * 32 * POS))
-    g = lax.psum_scatter(jnp.concatenate([g[:9 * C].reshape(32, 72, C), g[9 * C:].reshape(32, 24, C)], axis=1).reshape(12 * C, C),
-                         "seq", scatter_dimension=0, tiled=True)
-    g = lax.psum(g, "dp") * scale
-    return vg.reshape(video.shape), g[:72], g[72:]
+    count = lax.axis_size("dp") * lax.axis_size("seq") * POS
+    vg, sg, tg = compute(video.reshape(POS, C), cotangent.reshape(POS, C),
+                         spatial_weight.reshape(3, 3 * C, C), temporal_weight, count ** -0.5)
+    return vg.reshape(video.shape), sg, tg
 
 
 def solution(mesh):

time: 271 us -> 73.3 us (0.27); the launches traced: 267 us -> 72 us
  waiting for transfers between devices: 198 us -> 0 us
  Pallas kernels: 46.3 us -> 67.6 us
  between operations: 14.1 us -> 0.66 us
  other arithmetic: 2.98 us -> 0 us
    reduce_scatter x1 -> x0, waiting for transfers between devices: 120 us -> none  [shards(): lax.psum_scatter(jnp.concatenate([g[:9 * C].reshape(32, 72, C), g[9 * C:]...]
    psum x1 -> x0, waiting for transfers between devices: 77.6 us -> none  [shards(): g = lax.psum(g, 'dp') * scale]
    pallas_call x1, Pallas kernels: 46.3 us -> 67.6 us  [compute(): pl.pallas_call(functools.partial(body, scale), name='halo_conv', out_shap...]
    slice x4 -> x0, local copies, waits for them, and re-layouts: 4.25 us -> none  [the longest x1 1.82 us: shards(): g[:9 * C].reshape(32, 72, C)]
  transfers between devices with their start and end apart: 2 -> 0, of which waited for: 2 -> 0; matrix products, arithmetic and copies ran while one was open for 0% -> 0% of each run, Pallas kernels for 0% -> 0%
where the time goes in v2:
time: 73.3 us; the launch traced here: 72 us
  Pallas kernels  67.6 us (92%)
  local copies, waits for them, and re-layouts  3.74 us (5%)
    pallas_call x1, Pallas kernels, compute(): pl.pallas_call(functools.partial(body, scale), name='halo_conv', out_shap...  67.6 us
    unnamed x7, local copies, waits for them, and re-layouts  3.74 us

profile of v2, /device:TPU:1, one launch (start us, length us, event | category | flops | bytes accessed | tf_op | source)
XLA Modules:
  0.0 72.0 jit_solution(5792634404928859715)
XLA Ops:
  0.6 67.6 %halo_conv.1 = (bf16[2560,256]{1,0:T(8,128)(2,1)}, f32[72,256]{1,0:T(8,128)}, f32[24,256]{1,0:T(8,128)}) custom-call(bf16[2560,256]{1,0:T(8,128)(2,1)} %bitcast.4, bf16[2560,256]{1,0:T(8,128)(2,1)} %bitcast.5, bf16[3,768,256]{2,1,0:T(8,128)(2,1)} %bitcast.7, bf16[3,256,256]{2,1,0:T(8,128)(2,1)} %tw_ref.1), custom_call_target="tpu_custom_call" | custom-call | tf_op jit(solution)/shard_map/halo_conv/pallas_call | solution.py:319
  68.2 0.0 copy-start
  68.2 0.0 copy-start.1
  68.2 2.5 %copy.10 = bf16[1,1,16,160,256]{4,3,2,1,0:T(8,128)(2,1)} copy(bf16[1,1,16,160,256]{4,3,2,1,0:T(8,128)(2,1)} %bitcast.6) | data formatting | bytes 2621440
  70.7 0.0 copy-done
  70.7 0.6 copy.11
  71.4 0.0 copy-done.1
  71.4 0.6 copy.12
Async XLA Ops:
  68.2 2.5 %copy-start = (f32[72,256]{1,0:T(8,128)S(1)}, f32[72,256]{1,0:T(8,128)}, u32[]{:S(2)}) copy-start(f32[72,256]{1,0:T(8,128)} %get-tuple-element.13) | copy-start | bytes 221188
  68.2 3.1 %copy-start.1 = (f32[24,256]{1,0:T(8,128)S(1)}, f32[24,256]{1,0:T(8,128)}, u32[]{:S(2)}) copy-start(f32[24,256]{1,0:T(8,128)} %get-tuple-element.14) | copy-start | bytes 73732

commit v3 on v1

v3 whole, which is shorter than its diff:
```python
import functools

import jax
import jax.numpy as jnp
from jax import lax
from jax.experimental import pallas as pl
from jax.experimental.pallas import tpu as pltpu
from jax.sharding import PartitionSpec as P

MESH = pl.DeviceIdType.MESH
H, W, C = 16, 160, 256
HALF = C // 2
POS = H * W
NQ = 8
RQ = POS // NQ
F32, BF16 = jnp.float32, jnp.bfloat16
PLANE = [(dx, dy) for dx in range(4) for dy in range(4) if dx or dy]
SETS = ((0, 5), (5, 10), (10, 16))


def dot(a, b):
    return lax.dot_general(a, b, (((1,), (0,)), ((), ())), preferred_element_type=F32)


def shifted(x):
    n = x.shape[0]
    col = lax.broadcasted_iota(jnp.int32, x.shape, 0) % W
    before = jnp.where(col == 0, 0.0, pltpu.roll(x, 1, 0))
    after = jnp.where(col == W - 1, 0.0, pltpu.roll(x, n - 1, 0))
    return before, after


def body(scale, stop, v_hbm, c_hbm, sw_hbm, tw_hbm, vg_ref, sg_ref, tg_ref,
         v_ref, sw_ref, tw_ref, vcat, hgcat, cots, v_t, a_t, dsil, sw_t, tw_t, g_ref,
         pair_out, pair_in, s1_out, s1_in, s2_out, s2_in, last_out, last_in,
         far_send, far_recv, near_send, near_recv, pair_send, pair_recv, s1_send, s1_recv,
         s2_send, s2_recv, last_send, last_recv, in_sems):
    dp, seq = lax.axis_index("dp"), lax.axis_index("seq")
    n_seq = lax.axis_size("seq")
    core = lax.rem(seq, 2)
    x, y_lo = dp // 2, lax.rem(dp, 2)
    z, y_hi = seq // 4, lax.rem(seq // 2, 2)
    y = 2 * y_hi + y_lo
    sibling = seq + 1 - 2 * core
    prev = lax.rem(seq + n_seq - 2, n_seq)
    following = lax.rem(seq + 2, n_seq)

    def place(dx, dy, dz):
        to_x, to_y, to_z = (x + dx) & 3, (y + dy) & 3, (z + dz) & 7
        return (2 * to_x + (to_y & 1), 4 * to_z + (to_y & 2) + core)

    def rows(q):
        return pl.ds(pl.multiple_of(q * RQ, RQ), RQ)

    def inner(q):
        return pl.ds(pl.multiple_of(W + q * RQ, W), RQ)

    def remote(src, dst, send, recv, device):
        return pltpu.make_async_remote_copy(
            src_ref=src, dst_ref=dst, send_sem=send, recv_sem=recv, device_id=device, device_id_type=MESH)

    def far(q):
        return remote(c_hbm.at[rows(q)], cots.at[rows(q), pl.ds(2 * C, C)],
                      far_send.at[q], far_recv.at[q], {"seq": prev})

    def near_own(q):
        return remote(c_hbm.at[rows(q)], cots.at[rows(q), pl.ds(C, C)],
                      near_send.at[q], near_recv.at[q], {"seq": sibling})

    def near_pass(q):
        return remote(cots.at[rows(q), pl.ds(2 * C, C)], cots.at[rows(q), pl.ds(C, C)],
                      near_send.at[q], near_recv.at[q], {"seq": sibling})

    barrier = pltpu.get_barrier_semaphore()
    for other in (following, sibling):
        pl.semaphore_signal(barrier, inc=1, device_id={"seq": other}, device_id_type=MESH)
    for dx, dy in PLANE:
        pl.semaphore_signal(barrier, inc=1, device_id=place(dx, dy, 0), device_id_type=MESH)
    for dz in range(1, 8):
        pl.semaphore_signal(barrier, inc=1, device_id=place(0, 0, dz), device_id_type=MESH)
    loads = [pltpu.make_async_copy(v_hbm, v_ref, in_sems.at[0]),
             pltpu.make_async_copy(sw_hbm, sw_ref, in_sems.at[1]),
             pltpu.make_async_copy(tw_hbm, tw_ref, in_sems.at[2]),
             pltpu.make_async_copy(c_hbm, cots.at[:, pl.ds(0, C)], in_sems.at[3])]
    for load in loads:
        load.start()
    pl.semaphore_wait(barrier, 24)
    if stop == "b":
        for load in loads:
            load.wait()
        return
    for q in range(NQ):
        far(q).start()

    @pl.when(core == 1)
    def _():
        for q in range(NQ):
            near_own(q).start()

    zero = jnp.zeros((W, 3 * C), BF16)
    for ref in (vcat, hgcat):
        ref[0:W, :] = zero
        ref[W + POS:2 * W + POS, :] = zero
    loads[0].wait()

    def spread(q, _):
        v = v_ref[rows(q), :]
        before, after = shifted(v.astype(F32))
        vcat[inner(q), 0:C] = before.astype(BF16)
        vcat[inner(q), C:2 * C] = v
        vcat[inner(q), 2 * C:] = after.astype(BF16)
        return 0
    lax.fori_loop(0, NQ, spread, 0)
    loads[1].wait()

    def forward(q, _):
        acc = jnp.zeros((RQ, C), F32)
        for a in range(3):
            acc = acc + dot(vcat[pl.ds(pl.multiple_of(q * RQ + a * W, W), RQ), :], sw_ref[a])
        v = acc.astype(BF16).astype(F32)
        s = 1.0 / (1.0 + jnp.exp(-v))
        dsil[rows(q), :] = s * (1.0 + v * (1.0 - s))
        hgcat[inner(q), 0:C] = (v * s).astype(BF16)
        return 0
    lax.fori_loop(0, NQ, forward, 0)
    for m in range(POS // C):
        a_t[:, m * C:(m + 1) * C] = hgcat[W + m * C:W + (m + 1) * C, 0:C].T
        v_t[:, m * C:(m + 1) * C] = v_ref[m * C:(m + 1) * C, :].T

    loads[2].wait()
    lives = [(seq + k < n_seq).astype(F32) for k in range(3)]
    for a in range(3):
        for b in range(3):
            sw_t[a, b * C:(b + 1) * C, :] = sw_ref[a, b * C:(b + 1) * C, :].T
        tw_t[a * C:(a + 1) * C, :] = (tw_ref[a].astype(F32) * lives[a]).astype(BF16).T
    loads[3].wait()

    if stop == "h":
        def halo_only(q, _):
            far(q).wait_recv()

            @pl.when(core == 0)
            def _():
                near_pass(q).start()
            near_own(q).wait_recv()
            return 0
        lax.fori_loop(0, NQ, halo_only, 0)
        def drain(q, _):
            far(q).wait_send()
            near_own(q).wait_send()
            return 0
        lax.fori_loop(0, NQ, drain, 0)
        return

    def chunk(q, _):
        far(q).wait_recv()

        @pl.when(core == 0)
        def _():
            near_pass(q).start()
        near_own(q).wait_recv()
        hg = (dot(cots[rows(q), :], tw_t[...]) * dsil[rows(q), :]).astype(BF16)
        before, after = shifted(hg.astype(F32))
        hgcat[inner(q), 0:C] = after.astype(BF16)
        hgcat[inner(q), C:2 * C] = hg
        hgcat[inner(q), 2 * C:] = before.astype(BF16)
        return 0

    def back(q, _):
        acc = jnp.zeros((RQ, C), F32)
        for a in range(3):
            acc = acc + dot(hgcat[pl.ds(pl.multiple_of(q * RQ + (2 - a) * W, W), RQ), :], sw_t[a])
        vg_ref[rows(q), :] = acc.astype(BF16)
        return 0

    def chunk_back(q, _):
        chunk(q, 0)
        back(q - 1, 0)
        return 0

    def put(first, index, part):
        for b in range(3):
            where = pl.ds(pl.multiple_of((index * 3 + b) * C, C), C)
            value = part[:, b * C:(b + 1) * C]
            g_ref[where, :] = value if first else g_ref[where, :] + value

    def spatial(start, size, first):
        def tap(a, _):
            from_row = pl.multiple_of(start + (2 - a) * W, 32)
            put(first, a, dot(v_t[:, start:start + size], hgcat[pl.ds(from_row, size), :]))
            return 0
        return tap

    def temporal(start, size, first):
        part = dot(a_t[:, start:start + size], cots[start:start + size, :])
        put(first, 3, jnp.concatenate([part[:, k * C:(k + 1) * C] * lives[k] for k in range(3)], axis=1))

    chunk(0, 0)
    lax.fori_loop(1, 4, chunk_back, 0)
    lax.fori_loop(0, 3, spatial(0, 1024, True), 0)
    temporal(0, 1280, True)
    lax.fori_loop(4, 6, chunk_back, 0)
    lax.fori_loop(0, 3, spatial(1024, 512, False), 0)
    temporal(1280, 512, False)
    chunk_back(6, 0)
    lax.fori_loop(0, 3, spatial(1536, 512, False), 0)
    temporal(1792, 256, False)
    chunk(7, 0)
    temporal(2048, 512, False)

    def block(g, parity):
        return 144 * g + 72 * parity, 9 * C + 48 * g + 24 * parity

    def give(g):
        s_row, t_row = block(g, 1 - core)
        pair_out[g, 0:72, :] = g_ref[pl.ds(pl.multiple_of(s_row, 8), 72), :].astype(BF16)
        pair_out[g, 72:96, :] = g_ref[pl.ds(pl.multiple_of(t_row, 8), 24), :].astype(BF16)

    def pair(n):
        g0, g1 = SETS[n]
        return remote(pair_out.at[g0:g1], pair_in.at[g0:g1], pair_send.at[n], pair_recv.at[n], {"seq": sibling})

    final_tap = spatial(2048, 512, False)
    for n in range(3):
        final_tap(n, 0)
        for g in range(*SETS[n]):
            give(g)
        pair(n).start()
    back(6, 0)

    def finish(*copies):
        for n in range(3):
            pair(n).wait_send()
        for copy in copies:
            copy.wait_send()

        def drain(q, _):
            far(q).wait_send()
            near_own(q).wait_send()
            return 0
        lax.fori_loop(0, NQ, drain, 0)

    def whole(ref, sends, recvs, n):
        return remote(ref, ref, sends.at[n], recvs.at[n], {"seq": sibling})

    def take(r):
        for h in range(8):
            s, t = [], []
            for g in (2 * h, 2 * h + 1):
                s_row, t_row = block(g, core)
                s.append(g_ref[pl.ds(pl.multiple_of(s_row + 24 * r, 8), 24), :]
                         + pair_in[g, 24 * r:24 * r + 24, :].astype(F32))
                t.append(g_ref[pl.ds(pl.multiple_of(t_row + 8 * r, 8), 8), :]
                         + pair_in[g, 72 + 8 * r:80 + 8 * r, :].astype(F32))
            for q in range(4):
                value = jnp.concatenate([i[8 * q:8 * q + 8] for i in s] if q < 3 else t, axis=0).astype(BF16)
                for part in range(2):
                    s1_out[r, part, q, 16 * h:16 * h + 16, :] = value[:, part * HALF:(part + 1) * HALF]

    def s1(r, part, d):
        to = ((y if part else x) + d) & 3
        return remote(s1_out.at[r, part, to], s1_in.at[r, part, d - 1], s1_send.at[r], s1_recv.at[r],
                      place(0, d, 0) if part else place(d, 0, 0))

    def s2(r, d):
        return remote(s2_out.at[r, pl.ds(pl.multiple_of(16 * ((z + d) & 7), 16), 16)], s2_in.at[r, d - 1],
                      s2_send.at[r], s2_recv.at[r], place(0, 0, d))

    me = 4 * x + y

    def last(r, dx, dy):
        return remote(last_out.at[r, ((y + dy) & 3) // 2], last_in.at[r, me], last_send.at[r], last_recv.at[r],
                      place(dx, dy, 0))

    s1_all = [whole(s1_in.at[r], s1_send, s1_recv, r) for r in range(3)]
    s2_all = [whole(s2_in.at[r], s2_send, s2_recv, r) for r in range(3)]
    last_all = [whole(last_in.at[r, 0:15], last_send, last_recv, r) for r in range(3)]
    for n in range(3):
        pair(n).wait_recv()
    if stop == "p":
        back(7, 0)
        finish()
        return
    for r in range(3):
        take(r)
        for d in (2, 1, 3):
            for part in range(2):
                s1(r, part, d).start()
    back(7, 0)
    for r in range(3):
        s1_all[r].wait_recv()
        for part, mine in ((0, x), (1, y)):
            total = s1_out[r, part, mine].astype(F32)
            for d in range(3):
                total = total + s1_in[r, part, d].astype(F32)
            s2_out[r, :, part * HALF:(part + 1) * HALF] = total.astype(BF16)
        for d in (4, 3, 5, 2, 6, 1, 7):
            s2(r, d).start()
    for r in range(3):
        s2_all[r].wait_recv()
        total = s2_out[r, pl.ds(pl.multiple_of(16 * z, 16), 16), :].astype(F32)
        for d in range(7):
            total = total + s2_in[r, d].astype(F32)
        for to in range(2):
            piece = total[8 * to:8 * to + 8]
            last_out[r, to, :, :] = jnp.concatenate([piece[:, :HALF], piece[:, HALF:]], axis=0).astype(BF16)
        for dx, dy in PLANE:
            last(r, dx, dy).start()
        last_in[r, me, :, :] = last_out[r, y_hi]
    for r in range(3):
        last_all[r].wait_recv()
        for q in range(4):
            left = last_in[r, 4 * q, 0:8, :].astype(F32)
            right = last_in[r, q, 8:16, :].astype(F32)
            for k in range(1, 4):
                left = left + last_in[r, 4 * q + k, 0:8, :].astype(F32)
                right = right + last_in[r, 4 * k + q, 8:16, :].astype(F32)
            out, row = (sg_ref, 24 * r + 8 * q) if q < 3 else (tg_ref, 8 * r)
            out[row:row + 8, 0:HALF] = left * scale
            out[row:row + 8, HALF:] = right * scale
    finish(*s1_all, *s2_all, *last_all)


def hand_over(*refs):
    ins, outs, sems = refs[:3], refs[3:6], refs[6]
    views = [(0, pl.ds(n * RQ, RQ)) for n in range(NQ)] + [(1, pl.ds(0, 72)), (2, pl.ds(0, 24))]
    copies = [pltpu.make_async_copy(ins[i].at[w], outs[i].at[w], sems.at[n]) for n, (i, w) in enumerate(views)]
    for copy in copies:
        copy.start()
    for copy in copies:
        copy.wait()


def compute(v, c, sw, tw, scale, stop=None, cid=0):
    anywhere = pl.BlockSpec(memory_space=pl.ANY)
    vm = pl.BlockSpec(memory_space=pltpu.VMEM)
    dma = pltpu.SemaphoreType.DMA
    shapes = (jax.ShapeDtypeStruct((POS, C), BF16), jax.ShapeDtypeStruct((72, C), F32),
              jax.ShapeDtypeStruct((24, C), F32))
    grads = pl.pallas_call(
        functools.partial(body, scale, stop), name=f"block_grads{'' if stop is None else stop}",
        out_shape=tuple(pltpu.VMEM(t.shape, t.dtype) for t in shapes),
        in_specs=[anywhere] * 4, out_specs=(vm, vm, vm),
        scratch_shapes=[
            pltpu.VMEM((POS, C), BF16),
            pltpu.VMEM((3, 3 * C, C), BF16),
            pltpu.VMEM((3, C, C), BF16),
            pltpu.VMEM((POS + 2 * W, 3 * C), BF16),
            pltpu.VMEM((POS + 2 * W, 3 * C), BF16),
            pltpu.VMEM((POS, 3 * C), BF16),
            pltpu.VMEM((C, POS), BF16),
            pltpu.VMEM((C, POS), BF16),
            pltpu.VMEM((POS, C), F32),
            pltpu.VMEM((3, 3 * C, C), BF16),
            pltpu.VMEM((3 * C, C), BF16),
            pltpu.VMEM((12 * C, C), F32),
            pltpu.VMEM((16, 96, C), BF16), pltpu.VMEM((16, 96, C), BF16),
            pltpu.VMEM((3, 2, 4, 128, HALF), BF16), pltpu.VMEM((3, 2, 3, 128, HALF), BF16),
            pltpu.VMEM((3, 128, C), BF16), pltpu.VMEM((3, 7, 16, C), BF16),
            pltpu.VMEM((3, 2, 16, HALF), BF16), pltpu.VMEM((3, 16, 16, HALF), BF16),
        ] + [dma((NQ,))] * 4 + [dma((3,))] * 8 + [dma((4,))],
        compiler_params=pltpu.CompilerParams(
            collective_id=cid, has_side_effects=True, vmem_limit_bytes=56 * 2**20),
    )(v, c, sw, tw)
    return pl.pallas_call(
        hand_over, name="hand_over", out_shape=shapes,
        in_specs=[anywhere] * 3, out_specs=(anywhere,) * 3,
        scratch_shapes=[dma((NQ + 2,))],
    )(*[pltpu.with_memory_space_constraint(g, pltpu.VMEM) for g in grads])


def shards(video, cotangent, spatial_weight, temporal_weight):
    count = lax.axis_size("dp") * lax.axis_size("seq") * POS
    vg, sg, tg = compute(video.reshape(POS, C), cotangent.reshape(POS, C),
                         spatial_weight.reshape(3, 3 * C, C), temporal_weight, count ** -0.5)
    return vg.reshape(video.shape), sg, tg


def solution(mesh):
    placed = (P("dp", "seq", None, None, None), P("dp", "seq", None, None, None), P(), P())
    return jax.shard_map(
        shards, mesh=mesh, in_specs=placed,
        out_specs=(P("dp", "seq", None, None, None), P("seq", None), P("seq", None)),
        check_vma=False)
```

time: 271 us -> 63.3 us (0.23); the launches traced: 267 us -> 63.1 us
  waiting for transfers between devices: 198 us -> 0 us
  Pallas kernels: 46.3 us -> 62.4 us
  between operations: 14.1 us -> 0.64 us
  local copies, waits for them, and re-layouts: 5.31 us -> 0 us
  other arithmetic: 2.98 us -> 0 us
    reduce_scatter x1 -> x0, waiting for transfers between devices: 120 us -> none  [shards(): lax.psum_scatter(jnp.concatenate([g[:9 * C].reshape(32, 72, C), g[9 * C:]...]
    psum x1 -> x0, waiting for transfers between devices: 77.6 us -> none  [shards(): g = lax.psum(g, 'dp') * scale]
    pallas_call x1 -> x2, Pallas kernels: 46.3 us -> 62.4 us  [the longest x1 61.3 us: compute(): pl.pallas_call(functools.partial(body, scale, stop), name=f"block_grads{(...]
    slice x4 -> x0, local copies, waits for them, and re-layouts: 4.25 us -> none  [the longest x1 1.82 us: shards(): g[:9 * C].reshape(32, 72, C)]
  transfers between devices with their start and end apart: 2 -> 0, of which waited for: 2 -> 0; matrix products, arithmetic and copies ran while one was open for 0% -> 0% of each run, Pallas kernels for 0% -> 0%
where the time goes in v3:
time: 63.3 us; the launch traced here: 63.1 us
  Pallas kernels  62.4 us (99%)
  between operations  0.64 us (1%)
    pallas_call x1, Pallas kernels, compute(): pl.pallas_call(functools.partial(body, scale, stop), name=f"block_grads{(...  61.3 us

profile of v3, /device:TPU:1, one launch (start us, length us, event | category | flops | bytes accessed | tf_op | source)
XLA Modules:
  0.0 63.1 jit_solution(14711723482907995631)
XLA Ops:
  0.6 61.3 %block_grads.1 = (bf16[2560,256]{1,0:T(8,128)(2,1)S(1)}, f32[72,256]{1,0:T(8,128)S(1)}, f32[24,256]{1,0:T(8,128)S(1)}) custom-call(bf16[2560,256]{1,0:T(8,128)(2,1)} %bitcast.4, bf16[2560,256]{1,0:T(8,128)(2,1)} %bitcast.5, bf16[3,768,256]{2,1,0:T(8,128)(2,1)} %bitcast.6, bf16[3,256,256]{2,1,0:T(8,128)(2,1)} %tw_hbm.1), custom_call_target="tpu_custom_call" | custom-call | tf_op jit(solution)/shard_map/block_grads/pallas_call | solution.py:340
  61.9 1.2 %hand_over.1 = (bf16[2560,256]{1,0:T(8,128)(2,1)}, f32[72,256]{1,0:T(8,128)}, f32[24,256]{1,0:T(8,128)}) custom-call(bf16[2560,256]{1,0:T(8,128)(2,1)S(1)} %get-tuple-element.9.refs_0_, f32[72,256]{1,0:T(8,128)S(1)} %get-tuple-element.10.refs_1_, f32[24,256]{1,0:T(8,128)S(1)} %get-tuple-element.11.refs_2_), custom_call_target="tpu_custom_call" | custom-call | tf_op jit(solution)/shard_map/hand_over/pallas_call | solution.py:365

commit v4 on v3

v4 whole, which is shorter than its diff:
```python
import functools

import jax
import jax.numpy as jnp
from jax import lax
from jax.experimental import pallas as pl
from jax.experimental.pallas import tpu as pltpu
from jax.sharding import PartitionSpec as P

MESH = pl.DeviceIdType.MESH
H, W, C = 16, 160, 256
HALF = C // 2
POS = H * W
NQ = 8
RQ = POS // NQ
F32, BF16 = jnp.float32, jnp.bfloat16
PLANE = [(dx, dy) for dx in (2, 1, 3, 0) for dy in (2, 1, 3, 0) if dx or dy]
NP = 16
SETS = ((12, 16), (6, 12), (0, 6))


def dot(a, b):
    return lax.dot_general(a, b, (((1,), (0,)), ((), ())), preferred_element_type=F32)


def shifted(x):
    n = x.shape[0]
    col = lax.broadcasted_iota(jnp.int32, x.shape, 0) % W
    before = jnp.where(col == 0, 0.0, pltpu.roll(x, 1, 0))
    after = jnp.where(col == W - 1, 0.0, pltpu.roll(x, n - 1, 0))
    return before, after


def body(scale, heights, v_hbm, c_hbm, sw_hbm, tw_hbm, vg_ref, sg_ref, tg_ref,
         v_ref, sw_ref, tw_ref, vcat, hgcat, cots, v_t, a_t, dsil, sw_t, tw_t, g_ref,
         pair_out, pair_in, pair_t_out, pair_t_in, *more):
    n_sets = len(heights)
    s1_out, s1_in, s2_out, s2_in, last_out, last_in = (more[n_sets * i:n_sets * (i + 1)] for i in range(6))
    (far_send, far_recv, near_send, near_recv, pair_send, pair_recv, s1_send, s1_recv,
     s2_send, s2_recv, last_send, last_recv, in_sems, ready) = more[6 * n_sets:]
    offsets = [sum(heights[:r]) for r in range(n_sets)]
    dp, seq = lax.axis_index("dp"), lax.axis_index("seq")
    n_seq = lax.axis_size("seq")
    core = lax.rem(seq, 2)
    x, y_lo = dp // 2, lax.rem(dp, 2)
    z, y_hi = seq // 4, lax.rem(seq // 2, 2)
    y = 2 * y_hi + y_lo
    sibling = seq + 1 - 2 * core
    prev = lax.rem(seq + n_seq - 2, n_seq)
    following = lax.rem(seq + 2, n_seq)

    def place(dx, dy, dz):
        to_x, to_y, to_z = (x + dx) & 3, (y + dy) & 3, (z + dz) & 7
        return (2 * to_x + (to_y & 1), 4 * to_z + (to_y & 2) + core)

    def rows(q):
        return pl.ds(pl.multiple_of(q * RQ, RQ), RQ)

    def inner(q):
        return pl.ds(pl.multiple_of(W + q * RQ, W), RQ)

    def lines(p, n=1):
        return pl.ds(pl.multiple_of(p * W, W), n * W)

    def remote(src, dst, send, recv, device):
        return pltpu.make_async_remote_copy(
            src_ref=src, dst_ref=dst, send_sem=send, recv_sem=recv, device_id=device, device_id_type=MESH)

    def far(p):
        return remote(c_hbm.at[lines(p)], cots.at[lines(p), pl.ds(2 * C, C)],
                      far_send.at[p], far_recv.at[p], {"seq": prev})

    def near_own(p):
        return remote(c_hbm.at[lines(p)], cots.at[lines(p), pl.ds(C, C)],
                      near_send.at[p], near_recv.at[p], {"seq": sibling})

    def near_pass(p):
        return remote(cots.at[lines(p), pl.ds(2 * C, C)], cots.at[lines(p), pl.ds(C, C)],
                      near_send.at[p], near_recv.at[p], {"seq": sibling})

    ahead = (place(1, 0, 0), place(0, 1, 0), place(0, 0, 1))
    behind = (place(3, 0, 0), place(0, 3, 0), place(0, 0, 7))

    def greet(sem, devices):
        for device in devices:
            pl.semaphore_signal(sem, inc=1, device_id=device, device_id_type=MESH)

    barrier = pltpu.get_barrier_semaphore()
    greet(barrier, ({"seq": following}, {"seq": sibling}) + ahead)
    loads = [pltpu.make_async_copy(v_hbm, v_ref, in_sems.at[0]),
             pltpu.make_async_copy(sw_hbm, sw_ref, in_sems.at[1]),
             pltpu.make_async_copy(tw_hbm, tw_ref, in_sems.at[2]),
             pltpu.make_async_copy(c_hbm, cots.at[:, pl.ds(0, C)], in_sems.at[3])]
    for load in loads:
        load.start()
    pl.semaphore_wait(barrier, 5)
    @pl.when(core == 0)
    def _():
        for p in range(NP):
            far(p).start()

    @pl.when(core == 1)
    def _():
        for p in range(NP):
            near_own(p).start()
    greet(ready.at[0], behind)

    zero = jnp.zeros((W, 3 * C), BF16)
    for ref in (vcat, hgcat):
        ref[0:W, :] = zero
        ref[W + POS:2 * W + POS, :] = zero
    loads[0].wait()

    def spread(q, _):
        v = v_ref[rows(q), :]
        before, after = shifted(v.astype(F32))
        vcat[inner(q), 0:C] = before.astype(BF16)
        vcat[inner(q), C:2 * C] = v
        vcat[inner(q), 2 * C:] = after.astype(BF16)
        return 0
    lax.fori_loop(0, NQ, spread, 0)
    @pl.when(core == 1)
    def _():
        for p in range(NP):
            far(p).start()
    loads[1].wait()
    pl.semaphore_wait(ready.at[0], 3)
    greet(ready.at[1], ahead + behind)

    def forward(q, _):
        acc = jnp.zeros((RQ, C), F32)
        for a in range(3):
            acc = acc + dot(vcat[pl.ds(pl.multiple_of(q * RQ + a * W, W), RQ), :], sw_ref[a])
        v = acc.astype(BF16).astype(F32)
        s = 1.0 / (1.0 + jnp.exp(-v))
        dsil[rows(q), :] = s * (1.0 + v * (1.0 - s))
        hgcat[inner(q), 0:C] = (v * s).astype(BF16)
        return 0
    lax.fori_loop(0, NQ, forward, 0)
    for m in range(POS // C):
        a_t[:, m * C:(m + 1) * C] = hgcat[W + m * C:W + (m + 1) * C, 0:C].T
        v_t[:, m * C:(m + 1) * C] = v_ref[m * C:(m + 1) * C, :].T

    pl.semaphore_wait(ready.at[1], 6)
    greet(ready.at[2], ahead + behind)

    loads[2].wait()
    lives = [(seq + k < n_seq).astype(F32) for k in range(3)]
    for a in range(3):
        for b in range(3):
            sw_t[a, b * C:(b + 1) * C, :] = sw_ref[a, b * C:(b + 1) * C, :].T
        tw_t[a * C:(a + 1) * C, :] = (tw_ref[a].astype(F32) * lives[a]).astype(BF16).T
    loads[3].wait()
    pl.semaphore_wait(ready.at[2], 6)
    greet(ready.at[3], ahead + behind)

    def chunk(p, n):
        for i in range(n):
            far(p + i).wait_recv()

            @pl.when(core == 0)
            def _():
                near_pass(p + i).start()
        for i in range(n):
            near_own(p + i).wait_recv()
        hg = (dot(cots[lines(p, n), :], tw_t[...]) * dsil[lines(p, n), :]).astype(BF16)
        before, after = shifted(hg.astype(F32))
        hgcat[lines(p + 1, n), 0:C] = after.astype(BF16)
        hgcat[lines(p + 1, n), C:2 * C] = hg
        hgcat[lines(p + 1, n), 2 * C:] = before.astype(BF16)

    def back(q, _):
        acc = jnp.zeros((RQ, C), F32)
        for a in range(3):
            acc = acc + dot(hgcat[pl.ds(pl.multiple_of(q * RQ + (2 - a) * W, W), RQ), :], sw_t[a])
        vg_ref[rows(q), :] = acc.astype(BF16)
        return 0

    def chunk_back(q, _):
        chunk(2 * q, 2)
        back(q - 1, 0)
        return 0

    def put(first, index, part):
        for b in range(3):
            where = pl.ds(pl.multiple_of((index * 3 + b) * C, C), C)
            value = part[:, b * C:(b + 1) * C]
            g_ref[where, :] = value if first else g_ref[where, :] + value

    def spatial(start, size, first):
        def tap(a, _):
            from_row = pl.multiple_of(start + (2 - a) * W, 32)
            put(first, a, dot(v_t[:, start:start + size], hgcat[pl.ds(from_row, size), :]))
            return 0
        return tap

    def temporal(start, size, first):
        part = dot(a_t[:, start:start + size], cots[start:start + size, :])
        put(first, 3, jnp.concatenate([part[:, k * C:(k + 1) * C] * lives[k] for k in range(3)], axis=1))

    chunk(0, 2)
    lax.fori_loop(1, 4, chunk_back, 0)
    lax.fori_loop(0, 3, spatial(0, 1024, True), 0)
    temporal(0, 1280, True)
    pl.semaphore_wait(ready.at[3], 6)
    lax.fori_loop(4, 6, chunk_back, 0)
    lax.fori_loop(0, 3, spatial(1024, 512, False), 0)
    temporal(1280, 512, False)
    chunk_back(6, 0)
    lax.fori_loop(0, 3, spatial(1536, 512, False), 0)
    temporal(1792, 256, False)
    def block(g, parity):
        return 144 * g + 72 * parity, 9 * C + 48 * g + 24 * parity

    def pair(n):
        g0, g1 = SETS[n]
        return remote(pair_out.at[g0:g1], pair_in.at[g0:g1], pair_send.at[n], pair_recv.at[n], {"seq": sibling})

    def give(n):
        for g in range(*SETS[n]):
            s_row, _ = block(g, 1 - core)
            pair_out[g, :, :] = g_ref[pl.ds(pl.multiple_of(s_row, 8), 72), :].astype(BF16)
        pair(n).start()

    pair_t = remote(pair_t_out, pair_t_in, pair_send.at[3], pair_recv.at[3], {"seq": sibling})
    chunk(14, 1)
    spatial(2048, 512, False)(2, 0)
    give(0)
    spatial(2048, 256, False)(1, 0)
    spatial(2048, 128, False)(0, 0)
    temporal(2048, 256, False)
    chunk(15, 1)
    spatial(2304, 256, False)(1, 0)
    give(1)
    temporal(2304, 256, False)
    for h in range(8):
        t_rows = [pl.ds(pl.multiple_of(block(g, 1 - core)[1], 8), 24) for g in (2 * h, 2 * h + 1)]
        pair_t_out[48 * h:48 * h + 48, :] = jnp.concatenate([g_ref[t, :] for t in t_rows], axis=0).astype(BF16)
    pair_t.start()
    spatial(2176, 256, False)(0, 0)
    give(2)

    def finish(*copies):
        for n in range(3):
            pair(n).wait_send()
        pair_t.wait_send()
        for copy in copies:
            copy.wait_send()

        def drain(p, _):
            far(p).wait_send()
            near_own(p).wait_send()
            return 0
        lax.fori_loop(0, NP, drain, 0)

    def whole(ref, sends, recvs, n):
        return remote(ref, ref, sends.at[n], recvs.at[n], {"seq": sibling})

    def take(r, n):
        high, off = heights[r], offsets[r]
        for h in range(SETS[n][0] // 2, SETS[n][1] // 2):
            s, t = [], []
            for g in (2 * h, 2 * h + 1):
                s_row, t_row = block(g, core)
                s.append(g_ref[pl.ds(pl.multiple_of(s_row + 3 * off, 8), 3 * high), :]
                         + pair_in[g, 3 * off:3 * off + 3 * high, :].astype(F32))
                t.append(g_ref[pl.ds(pl.multiple_of(t_row + off, 8), high), :]
                         + pair_t_in[24 * g + off:24 * g + off + high, :].astype(F32))
            for q in range(4):
                pieces = [i[high * q:high * q + high] for i in s] if q < 3 else t
                value = jnp.concatenate(pieces, axis=0).astype(BF16)
                for part in range(2):
                    s1_out[r][part, q, 2 * high * h:2 * high * (h + 1), :] = value[:, part * HALF:(part + 1) * HALF]

    def s1(r, part, d):
        to = ((y if part else x) + d) & 3
        return remote(s1_out[r].at[part, to], s1_in[r].at[part, d - 1], s1_send.at[r], s1_recv.at[r],
                      place(0, d, 0) if part else place(d, 0, 0))

    def of_z(r, at):
        return pl.ds(pl.multiple_of(2 * heights[r] * at, 16), 2 * heights[r])

    def s2(r, d):
        return remote(s2_out[r].at[of_z(r, (z + d) & 7)], s2_in[r].at[d - 1],
                      s2_send.at[r], s2_recv.at[r], place(0, 0, d))

    me = 4 * x + y

    def last(r, dx, dy):
        return remote(last_out[r].at[((y + dy) & 3) // 2], last_in[r].at[me], last_send.at[r], last_recv.at[r],
                      place(dx, dy, 0))

    s1_all = [whole(s1_in[r], s1_send, s1_recv, r) for r in range(n_sets)]
    s2_all = [whole(s2_in[r], s2_send, s2_recv, r) for r in range(n_sets)]
    last_all = [whole(last_in[r].at[0:15], last_send, last_recv, r) for r in range(n_sets)]
    back(6, 0)
    pair_t.wait_recv()
    for n in range(2):
        pair(n).wait_recv()
        for r in range(n_sets):
            take(r, n)
    pair(2).wait_recv()
    for r in range(n_sets):
        take(r, 2)
        for d in (2, 1, 3):
            for part in range(2):
                s1(r, part, d).start()
    back(7, 0)
    for r in range(n_sets):
        s1_all[r].wait_recv()
        for part, mine in ((0, x), (1, y)):
            total = s1_out[r][part, mine].astype(F32)
            for d in range(3):
                total = total + s1_in[r][part, d].astype(F32)
            s2_out[r][:, part * HALF:(part + 1) * HALF] = total.astype(BF16)
        for d in (4, 3, 5, 2, 6, 1, 7):
            s2(r, d).start()
    for r in range(n_sets):
        high = heights[r]
        s2_all[r].wait_recv()
        total = s2_out[r][of_z(r, z), :].astype(F32)
        for d in range(7):
            total = total + s2_in[r][d].astype(F32)
        for to in range(2):
            piece = total[high * to:high * to + high]
            last_out[r][to, :, :] = jnp.concatenate([piece[:, :HALF], piece[:, HALF:]], axis=0).astype(BF16)
        for dx, dy in PLANE:
            last(r, dx, dy).start()
        last_in[r][me, :, :] = last_out[r][y_hi]
    for r in range(n_sets):
        high, off = heights[r], offsets[r]
        last_all[r].wait_recv()
        for q in range(4):
            left = last_in[r][4 * q, 0:high, :].astype(F32)
            right = last_in[r][q, high:2 * high, :].astype(F32)
            for k in range(1, 4):
                left = left + last_in[r][4 * q + k, 0:high, :].astype(F32)
                right = right + last_in[r][4 * k + q, high:2 * high, :].astype(F32)
            out, row = (sg_ref, 3 * off + high * q) if q < 3 else (tg_ref, off)
            out[row:row + high, 0:HALF] = left * scale
            out[row:row + high, HALF:] = right * scale
    finish(*s1_all, *s2_all, *last_all)


def hand_over(*refs):
    ins, outs, sems = refs[:3], refs[3:6], refs[6]
    views = [(0, pl.ds(n * RQ, RQ)) for n in range(NQ)] + [(1, pl.ds(0, 72)), (2, pl.ds(0, 24))]
    copies = [pltpu.make_async_copy(ins[i].at[w], outs[i].at[w], sems.at[n]) for n, (i, w) in enumerate(views)]
    for copy in copies:
        copy.start()
    for copy in copies:
        copy.wait()


def compute(v, c, sw, tw, scale):
    heights = (8, 8, 8)
    anywhere = pl.BlockSpec(memory_space=pl.ANY)
    vm = pl.BlockSpec(memory_space=pltpu.VMEM)
    dma = pltpu.SemaphoreType.DMA
    shapes = (jax.ShapeDtypeStruct((POS, C), BF16), jax.ShapeDtypeStruct((72, C), F32),
              jax.ShapeDtypeStruct((24, C), F32))
    grads = pl.pallas_call(
        functools.partial(body, scale, heights), name="block_grads",
        out_shape=tuple(pltpu.VMEM(t.shape, t.dtype) for t in shapes),
        in_specs=[anywhere] * 4, out_specs=(vm, vm, vm),
        scratch_shapes=[
            pltpu.VMEM((POS, C), BF16),
            pltpu.VMEM((3, 3 * C, C), BF16),
            pltpu.VMEM((3, C, C), BF16),
            pltpu.VMEM((POS + 2 * W, 3 * C), BF16),
            pltpu.VMEM((POS + 2 * W, 3 * C), BF16),
            pltpu.VMEM((POS, 3 * C), BF16),
            pltpu.VMEM((C, POS), BF16),
            pltpu.VMEM((C, POS), BF16),
            pltpu.VMEM((POS, C), F32),
            pltpu.VMEM((3, 3 * C, C), BF16),
            pltpu.VMEM((3 * C, C), BF16),
            pltpu.VMEM((12 * C, C), F32),
            pltpu.VMEM((16, 72, C), BF16), pltpu.VMEM((16, 72, C), BF16),
            pltpu.VMEM((384, C), BF16), pltpu.VMEM((384, C), BF16),
            *[pltpu.VMEM((2, 4, 16 * h, HALF), BF16) for h in heights],
            *[pltpu.VMEM((2, 3, 16 * h, HALF), BF16) for h in heights],
            *[pltpu.VMEM((16 * h, C), BF16) for h in heights],
            *[pltpu.VMEM((7, 2 * h, C), BF16) for h in heights],
            *[pltpu.VMEM((2, 2 * h, HALF), BF16) for h in heights],
            *[pltpu.VMEM((16, 2 * h, HALF), BF16) for h in heights],
        ] + [dma((NP,))] * 4 + [dma((4,))] * 2 + [dma((3,))] * 6 + [dma((4,)), pltpu.SemaphoreType.REGULAR((4,))],
        compiler_params=pltpu.CompilerParams(
            collective_id=0, has_side_effects=True, vmem_limit_bytes=56 * 2**20),
    )(v, c, sw, tw)
    return pl.pallas_call(
        hand_over, name="hand_over", out_shape=shapes,
        in_specs=[anywhere] * 3, out_specs=(anywhere,) * 3,
        scratch_shapes=[dma((NQ + 2,))],
    )(*[pltpu.with_memory_space_constraint(g, pltpu.VMEM) for g in grads])


def shards(video, cotangent, spatial_weight, temporal_weight):
    count = lax.axis_size("dp") * lax.axis_size("seq") * POS
    vg, sg, tg = compute(video.reshape(POS, C), cotangent.reshape(POS, C),
                         spatial_weight.reshape(3, 3 * C, C), temporal_weight, count ** -0.5)
    return vg.reshape(video.shape), sg, tg


def solution(mesh):
    placed = (P("dp", "seq", None, None, None), P("dp", "seq", None, None, None), P(), P())
    return jax.shard_map(
        shards, mesh=mesh, in_specs=placed,
        out_specs=(P("dp", "seq", None, None, None), P("seq", None), P("seq", None)),
        check_vma=False)
```

time: 63.3 us -> 63.3 us (level)
  no operation moved by 1% of the time
where the time goes in v4:
time: 63.3 us; the launch traced here: 63.2 us
  Pallas kernels  62.6 us (99%)
  between operations  0.64 us (1%)
    pallas_call x1, Pallas kernels, compute(): pl.pallas_call(functools.partial(body, scale, heights), name='block_grads...  61.4 us

profile of v4, /device:TPU:1, one launch (start us, length us, event | category | flops | bytes accessed | tf_op | source)
XLA Modules:
  0.0 63.2 jit_solution(3378731004622639832)
XLA Ops:
  0.6 61.4 %block_grads.1 = (bf16[2560,256]{1,0:T(8,128)(2,1)S(1)}, f32[72,256]{1,0:T(8,128)S(1)}, f32[24,256]{1,0:T(8,128)S(1)}) custom-call(bf16[2560,256]{1,0:T(8,128)(2,1)} %bitcast.4, bf16[2560,256]{1,0:T(8,128)(2,1)} %bitcast.5, bf16[3,768,256]{2,1,0:T(8,128)(2,1)} %bitcast.6, bf16[3,256,256]{2,1,0:T(8,128)(2,1)} %tw_hbm.1), custom_call_target="tpu_custom_call" | custom-call | tf_op jit(solution)/shard_map/block_grads/pallas_call | solution.py:362
  62.1 1.2 %hand_over.1 = (bf16[2560,256]{1,0:T(8,128)(2,1)}, f32[72,256]{1,0:T(8,128)}, f32[24,256]{1,0:T(8,128)}) custom-call(bf16[2560,256]{1,0:T(8,128)(2,1)S(1)} %get-tuple-element.9.refs_0_, f32[72,256]{1,0:T(8,128)S(1)} %get-tuple-element.10.refs_1_, f32[24,256]{1,0:T(8,128)S(1)} %get-tuple-element.11.refs_2_), custom_call_target="tpu_custom_call" | custom-call | tf_op jit(solution)/shard_map/hand_over/pallas_call | solution.py:391

commit v5 on v4

--- a/solution.py
+++ b/solution.py
@@ -14,7 +14,7 @@
 NQ = 8
 RQ = POS // NQ
 F32, BF16 = jnp.float32, jnp.bfloat16
-PLANE = [(dx, dy) for dx in (2, 1, 3, 0) for dy in (2, 1, 3, 0) if dx or dy]
+PLANE = [(dx, dy) for dx in range(4) for dy in range(4) if dx or dy]
 NP = 16
 SETS = ((12, 16), (6, 12), (0, 6))
 
@@ -94,10 +94,8 @@
     for load in loads:
         load.start()
     pl.semaphore_wait(barrier, 5)
-    @pl.when(core == 0)
-    def _():
-        for p in range(NP):
-            far(p).start()
+    for p in range(NP):
+        far(p).start()
 
     @pl.when(core == 1)
     def _():
@@ -119,10 +117,6 @@
         vcat[inner(q), 2 * C:] = after.astype(BF16)
         return 0
     lax.fori_loop(0, NQ, spread, 0)
-    @pl.when(core == 1)
-    def _():
-        for p in range(NP):
-            far(p).start()
     loads[1].wait()
     pl.semaphore_wait(ready.at[0], 3)
     greet(ready.at[1], ahead + behind)

time: 63.3 us -> 63.9 us (level)
  no operation moved by 1% of the time
where the time goes in v5:
time: 63.9 us; the launch traced here: 63.8 us
  Pallas kernels  63.2 us (99%)
  between operations  0.64 us (1%)
    pallas_call x1, Pallas kernels, compute(): pl.pallas_call(functools.partial(body, scale, heights), name='block_grads...  62 us

profile of v5, /device:TPU:1, one launch (start us, length us, event | category | flops | bytes accessed | tf_op | source)
XLA Modules:
  0.0 63.8 jit_solution(9460654716520095784)
XLA Ops:
  0.6 62.0 %block_grads.1 = (bf16[2560,256]{1,0:T(8,128)(2,1)S(1)}, f32[72,256]{1,0:T(8,128)S(1)}, f32[24,256]{1,0:T(8,128)S(1)}) custom-call(bf16[2560,256]{1,0:T(8,128)(2,1)} %bitcast.4, bf16[2560,256]{1,0:T(8,128)(2,1)} %bitcast.5, bf16[3,768,256]{2,1,0:T(8,128)(2,1)} %bitcast.6, bf16[3,256,256]{2,1,0:T(8,128)(2,1)} %tw_hbm.1), custom_call_target="tpu_custom_call" | custom-call | tf_op jit(solution)/shard_map/block_grads/pallas_call | solution.py:356
  62.6 1.2 %hand_over.1 = (bf16[2560,256]{1,0:T(8,128)(2,1)}, f32[72,256]{1,0:T(8,128)}, f32[24,256]{1,0:T(8,128)}) custom-call(bf16[2560,256]{1,0:T(8,128)(2,1)S(1)} %get-tuple-element.9.refs_0_, f32[72,256]{1,0:T(8,128)S(1)} %get-tuple-element.10.refs_1_, f32[24,256]{1,0:T(8,128)S(1)} %get-tuple-element.11.refs_2_), custom_call_target="tpu_custom_call" | custom-call | tf_op jit(solution)/shard_map/hand_over/pallas_call | solution.py:385

commit v6 on v4

--- a/solution.py
+++ b/solution.py
@@ -353,7 +353,7 @@
 
 
 def compute(v, c, sw, tw, scale):
-    heights = (8, 8, 8)
+    heights = (8, 16)
     anywhere = pl.BlockSpec(memory_space=pl.ANY)
     vm = pl.BlockSpec(memory_space=pltpu.VMEM)
     dma = pltpu.SemaphoreType.DMA

time: 63.3 us -> 64.4 us (1.017)
  Pallas kernels: 62.6 us -> 63.7 us
    pallas_call x1, Pallas kernels: 61.4 us -> 62.5 us  [compute(): pl.pallas_call(functools.partial(body, scale, heights), name='block_grads...]
where the time goes in v6:
time: 64.4 us; the launch traced here: 64.3 us
  Pallas kernels  63.7 us (99%)
    pallas_call x1, Pallas kernels, compute(): pl.pallas_call(functools.partial(body, scale, heights), name='block_grads...  62.5 us

profile of v6, /device:TPU:1, one launch (start us, length us, event | category | flops | bytes accessed | tf_op | source)
XLA Modules:
  0.0 64.3 jit_solution(15656741218822127103)
XLA Ops:
  0.6 62.5 %block_grads.1 = (bf16[2560,256]{1,0:T(8,128)(2,1)S(1)}, f32[72,256]{1,0:T(8,128)S(1)}, f32[24,256]{1,0:T(8,128)S(1)}) custom-call(bf16[2560,256]{1,0:T(8,128)(2,1)} %bitcast.4, bf16[2560,256]{1,0:T(8,128)(2,1)} %bitcast.5, bf16[3,768,256]{2,1,0:T(8,128)(2,1)} %bitcast.6, bf16[3,256,256]{2,1,0:T(8,128)(2,1)} %tw_hbm.1), custom_call_target="tpu_custom_call" | custom-call | tf_op jit(solution)/shard_map/block_grads/pallas_call | solution.py:362
  63.2 1.2 %hand_over.1 = (bf16[2560,256]{1,0:T(8,128)(2,1)}, f32[72,256]{1,0:T(8,128)}, f32[24,256]{1,0:T(8,128)}) custom-call(bf16[2560,256]{1,0:T(8,128)(2,1)S(1)} %get-tuple-element.9.refs_0_, f32[72,256]{1,0:T(8,128)S(1)} %get-tuple-element.10.refs_1_, f32[24,256]{1,0:T(8,128)S(1)} %get-tuple-element.11.refs_2_), custom_call_target="tpu_custom_call" | custom-call | tf_op jit(solution)/shard_map/hand_over/pallas_call | solution.py:391

commit v7 on v3

--- a/solution.py
+++ b/solution.py
@@ -15,7 +15,8 @@
 RQ = POS // NQ
 F32, BF16 = jnp.float32, jnp.bfloat16
 PLANE = [(dx, dy) for dx in range(4) for dy in range(4) if dx or dy]
-SETS = ((0, 5), (5, 10), (10, 16))
+NP = 16
+SETS = ((0, 4), (4, 10), (10, 16))
 
 
 def dot(a, b):
@@ -34,7 +35,7 @@
          v_ref, sw_ref, tw_ref, vcat, hgcat, cots, v_t, a_t, dsil, sw_t, tw_t, g_ref,
          pair_out, pair_in, s1_out, s1_in, s2_out, s2_in, last_out, last_in,
          far_send, far_recv, near_send, near_recv, pair_send, pair_recv, s1_send, s1_recv,
-         s2_send, s2_recv, last_send, last_recv, in_sems):
+         s2_send, s2_recv, last_send, last_recv, in_sems, ready):
     dp, seq = lax.axis_index("dp"), lax.axis_index("seq")
     n_seq = lax.axis_size("seq")
     core = lax.rem(seq, 2)
@@ -55,47 +56,53 @@
     def inner(q):
         return pl.ds(pl.multiple_of(W + q * RQ, W), RQ)
 
+    def lines(p, n=1):
+        return pl.ds(pl.multiple_of(p * W, W), n * W)
+
     def remote(src, dst, send, recv, device):
         return pltpu.make_async_remote_copy(
             src_ref=src, dst_ref=dst, send_sem=send, recv_sem=recv, device_id=device, device_id_type=MESH)
 
-    def far(q):
-        return remote(c_hbm.at[rows(q)], cots.at[rows(q), pl.ds(2 * C, C)],
-                      far_send.at[q], far_recv.at[q], {"seq": prev})
-
-    def near_own(q):
-        return remote(c_hbm.at[rows(q)], cots.at[rows(q), pl.ds(C, C)],
-                      near_send.at[q], near_recv.at[q], {"seq": sibling})
-
-    def near_pass(q):
-        return remote(cots.at[rows(q), pl.ds(2 * C, C)], cots.at[rows(q), pl.ds(C, C)],
-                      near_send.at[q], near_recv.at[q], {"seq": sibling})
+    def far(p):
+        return remote(c_hbm.at[lines(p)], cots.at[lines(p), pl.ds(2 * C, C)],
+                      far_send.at[p], far_recv.at[p], {"seq": prev})
+
+    def near_own(p):
+        return remote(c_hbm.at[lines(p)], cots.at[lines(p), pl.ds(C, C)],
+                      near_send.at[p], near_recv.at[p], {"seq": sibling})
+
+    def near_pass(p):
+        return remote(cots.at[lines(p), pl.ds(2 * C, C)], cots.at[lines(p), pl.ds(C, C)],
+                      near_send.at[p], near_recv.at[p], {"seq": sibling})
+
+    ahead = (place(1, 0, 0), place(0, 1, 0), place(0, 0, 1))
+    behind = (place(3, 0, 0), place(0, 3, 0), place(0, 0, 7))
+
+    def greet(sem, devices):
+        for device in devices:
+            pl.semaphore_signal(sem, inc=1, device_id=device, device_id_type=MESH)
 
     barrier = pltpu.get_barrier_semaphore()
-    for other in (following, sibling):
-        pl.semaphore_signal(barrier, inc=1, device_id={"seq": other}, device_id_type=MESH)
-    for dx, dy in PLANE:
-        pl.semaphore_signal(barrier, inc=1, device_id=place(dx, dy, 0), device_id_type=MESH)
-    for dz in range(1, 8):
-        pl.semaphore_signal(barrier, inc=1, device_id=place(0, 0, dz), device_id_type=MESH)
+    greet(barrier, ({"seq": following}, {"seq": sibling}) + ahead)
     loads = [pltpu.make_async_copy(v_hbm, v_ref, in_sems.at[0]),
              pltpu.make_async_copy(sw_hbm, sw_ref, in_sems.at[1]),
              pltpu.make_async_copy(tw_hbm, tw_ref, in_sems.at[2]),
              pltpu.make_async_copy(c_hbm, cots.at[:, pl.ds(0, C)], in_sems.at[3])]
     for load in loads:
         load.start()
-    pl.semaphore_wait(barrier, 24)
+    pl.semaphore_wait(barrier, 5)
     if stop == "b":
         for load in loads:
             load.wait()
         return
-    for q in range(NQ):
-        far(q).start()
+    for p in range(NP):
+        far(p).start()
 
     @pl.when(core == 1)
     def _():
-        for q in range(NQ):
-            near_own(q).start()
+        for p in range(NP):
+            near_own(p).start()
+    greet(ready.at[0], behind)
 
     zero = jnp.zeros((W, 3 * C), BF16)
     for ref in (vcat, hgcat):
@@ -112,6 +119,8 @@
         return 0
     lax.fori_loop(0, NQ, spread, 0)
     loads[1].wait()
+    pl.semaphore_wait(ready.at[0], 3)
+    greet(ready.at[1], ahead + behind)
 
     def forward(q, _):
         acc = jnp.zeros((RQ, C), F32)
@@ -127,6 +136,9 @@
         a_t[:, m * C:(m + 1) * C] = hgcat[W + m * C:W + (m + 1) * C, 0:C].T
         v_t[:, m * C:(m + 1) * C] = v_ref[m * C:(m + 1) * C, :].T
 
+    pl.semaphore_wait(ready.at[1], 6)
+    greet(ready.at[2], ahead + behind)
+
     loads[2].wait()
     lives = [(seq + k < n_seq).astype(F32) for k in range(3)]
     for a in range(3):
@@ -134,37 +146,23 @@
             sw_t[a, b * C:(b + 1) * C, :] = sw_ref[a, b * C:(b + 1) * C, :].T
         tw_t[a * C:(a + 1) * C, :] = (tw_ref[a].astype(F32) * lives[a]).astype(BF16).T
     loads[3].wait()
-
-    if stop == "h":
-        def halo_only(q, _):
-            far(q).wait_recv()
+    pl.semaphore_wait(ready.at[2], 6)
+    greet(ready.at[3], ahead + behind)
+
+    def chunk(p, n):
+        for i in range(n):
+            far(p + i).wait_recv()
 
             @pl.when(core == 0)
             def _():
-                near_pass(q).start()
-            near_own(q).wait_recv()
-            return 0
-        lax.fori_loop(0, NQ, halo_only, 0)
-        def drain(q, _):
-            far(q).wait_send()
-            near_own(q).wait_send()
-            return 0
-        lax.fori_loop(0, NQ, drain, 0)
-        return
-
-    def chunk(q, _):
-        far(q).wait_recv()
-
-        @pl.when(core == 0)
-        def _():
-            near_pass(q).start()
-        near_own(q).wait_recv()
-        hg = (dot(cots[rows(q), :], tw_t[...]) * dsil[rows(q), :]).astype(BF16)
+                near_pass(p + i).start()
+        for i in range(n):
+            near_own(p + i).wait_recv()
+        hg = (dot(cots[lines(p, n), :], tw_t[...]) * dsil[lines(p, n), :]).astype(BF16)
         before, after = shifted(hg.astype(F32))
-        hgcat[inner(q), 0:C] = after.astype(BF16)
-        hgcat[inner(q), C:2 * C] = hg
-        hgcat[inner(q), 2 * C:] = before.astype(BF16)
-        return 0
+        hgcat[lines(p + 1, n), 0:C] = after.astype(BF16)
+        hgcat[lines(p + 1, n), C:2 * C] = hg
+        hgcat[lines(p + 1, n), 2 * C:] = before.astype(BF16)
 
     def back(q, _):
         acc = jnp.zeros((RQ, C), F32)
@@ -174,7 +172,7 @@
         return 0
 
     def chunk_back(q, _):
-        chunk(q, 0)
+        chunk(2 * q, 2)
         back(q - 1, 0)
         return 0
 
@@ -195,18 +193,21 @@
         part = dot(a_t[:, start:start + size], cots[start:start + size, :])
         put(first, 3, jnp.concatenate([part[:, k * C:(k + 1) * C] * lives[k] for k in range(3)], axis=1))
 
-    chunk(0, 0)
+    chunk(0, 2)
     lax.fori_loop(1, 4, chunk_back, 0)
     lax.fori_loop(0, 3, spatial(0, 1024, True), 0)
     temporal(0, 1280, True)
+    pl.semaphore_wait(ready.at[3], 6)
     lax.fori_loop(4, 6, chunk_back, 0)
     lax.fori_loop(0, 3, spatial(1024, 512, False), 0)
     temporal(1280, 512, False)
     chunk_back(6, 0)
     lax.fori_loop(0, 3, spatial(1536, 512, False), 0)
     temporal(1792, 256, False)
-    chunk(7, 0)
-    temporal(2048, 512, False)
+    chunk(14, 1)
+    temporal(2048, 256, False)
+    chunk(15, 1)
+    temporal(2304, 256, False)
 
     def block(g, parity):
         return 144 * g + 72 * parity, 9 * C + 48 * g + 24 * parity
@@ -234,17 +235,17 @@
         for copy in copies:
             copy.wait_send()
 
-        def drain(q, _):
-            far(q).wait_send()
-            near_own(q).wait_send()
+        def drain(p, _):
+            far(p).wait_send()
+            near_own(p).wait_send()
             return 0
-        lax.fori_loop(0, NQ, drain, 0)
+        lax.fori_loop(0, NP, drain, 0)
 
     def whole(ref, sends, recvs, n):
         return remote(ref, ref, sends.at[n], recvs.at[n], {"seq": sibling})
 
-    def take(r):
-        for h in range(8):
+    def take(r, n):
+        for h in range(SETS[n][0] // 2, SETS[n][1] // 2):
             s, t = [], []
             for g in (2 * h, 2 * h + 1):
                 s_row, t_row = block(g, core)
@@ -275,14 +276,17 @@
     s1_all = [whole(s1_in.at[r], s1_send, s1_recv, r) for r in range(3)]
     s2_all = [whole(s2_in.at[r], s2_send, s2_recv, r) for r in range(3)]
     last_all = [whole(last_in.at[r, 0:15], last_send, last_recv, r) for r in range(3)]
-    for n in range(3):
+    for n in range(2):
         pair(n).wait_recv()
+        for r in range(3):
+            take(r, n)
+    pair(2).wait_recv()
     if stop == "p":
         back(7, 0)
         finish()
         return
     for r in range(3):
-        take(r)
+        take(r, 2)
         for d in (2, 1, 3):
             for part in range(2):
                 s1(r, part, d).start()
@@ -358,7 +362,7 @@
             pltpu.VMEM((3, 2, 4, 128, HALF), BF16), pltpu.VMEM((3, 2, 3, 128, HALF), BF16),
             pltpu.VMEM((3, 128, C), BF16), pltpu.VMEM((3, 7, 16, C), BF16),
             pltpu.VMEM((3, 2, 16, HALF), BF16), pltpu.VMEM((3, 16, 16, HALF), BF16),
-        ] + [dma((NQ,))] * 4 + [dma((3,))] * 8 + [dma((4,))],
+        ] + [dma((NP,))] * 4 + [dma((3,))] * 8 + [dma((4,)), pltpu.SemaphoreType.REGULAR((4,))],
         compiler_params=pltpu.CompilerParams(
             collective_id=cid, has_side_effects=True, vmem_limit_bytes=56 * 2**20),
     )(v, c, sw, tw)

time: 63.3 us -> 63.3 us (level)
  no operation moved by 1% of the time
where the time goes in v7:
time: 63.3 us; the launch traced here: 63.2 us
  Pallas kernels  62.6 us (99%)
  between operations  0.64 us (1%)
    pallas_call x1, Pallas kernels, compute(): pl.pallas_call(functools.partial(body, scale, stop), name=f"block_grads{(...  61.5 us

profile of v7, /device:TPU:1, one launch (start us, length us, event | category | flops | bytes accessed | tf_op | source)
XLA Modules:
  0.0 63.2 jit_solution(8066932813694360589)
XLA Ops:
  0.6 61.5 %block_grads.1 = (bf16[2560,256]{1,0:T(8,128)(2,1)S(1)}, f32[72,256]{1,0:T(8,128)S(1)}, f32[24,256]{1,0:T(8,128)S(1)}) custom-call(bf16[2560,256]{1,0:T(8,128)(2,1)} %bitcast.4, bf16[2560,256]{1,0:T(8,128)(2,1)} %bitcast.5, bf16[3,768,256]{2,1,0:T(8,128)(2,1)} %bitcast.6, bf16[3,256,256]{2,1,0:T(8,128)(2,1)} %tw_hbm.1), custom_call_target="tpu_custom_call" | custom-call | tf_op jit(solution)/shard_map/block_grads/pallas_call | solution.py:344
  62.1 1.2 %hand_over.1 = (bf16[2560,256]{1,0:T(8,128)(2,1)}, f32[72,256]{1,0:T(8,128)}, f32[24,256]{1,0:T(8,128)}) custom-call(bf16[2560,256]{1,0:T(8,128)(2,1)S(1)} %get-tuple-element.9.refs_0_, f32[72,256]{1,0:T(8,128)S(1)} %get-tuple-element.10.refs_1_, f32[24,256]{1,0:T(8,128)S(1)} %get-tuple-element.11.refs_2_), custom_call_target="tpu_custom_call" | custom-call | tf_op jit(solution)/shard_map/hand_over/pallas_call | solution.py:369
